TPU v7x, 128 devices: a whole 4x4x4 slice. The times are simulated.
128 devices in a mesh: seq: 32 (over x, z_lo, y), dp: 4 (over z_hi, core).
Axes of the slice: x: 4, y: 4, z: 4 (z_hi: 2, z_lo: 2; z = z_hi * 2 + z_lo), core: 2. Of those that a mesh axis runs over, the one named last changes fastest.
Arguments:
- probe_matrix: bfloat16 [4, 4096, 4096], P('dp', 'seq'), may hold values from -150 to 150
- softmax_lookup_matrix: bfloat16 [4, 4096, 4096], P('dp', 'seq'), may hold values from -6 to 6
- acceptance_gate: bfloat16 [4, 4096, 4096], P('dp', 'seq'), may hold values from -6 to 6
- recurrent_lookup_matrix: bfloat16 [4, 4096, 4096], P('dp', 'seq'), may hold values from -6 to 6
- recurrent_payload_matrix: bfloat16 [4, 4096, 4096], P('dp', 'seq'), may hold values from -6 to 6
- upstream_adjoint: bfloat16 [4, 4096, 4096], P('dp', 'seq'), may hold values from -6 to 6
- feature_fading_exponent: float32 [32, 128], replicated, may hold values from -20 to -3
- diagonal_reward_factor: float32 [32, 128], replicated, may hold values from -6 to 6
- spike_fading_exponent: float32 [4, 4096, 32], P('dp', 'seq'), may hold values from -1 to 0, as said below
Outputs:
- grad_queries: bfloat16 [4, 4096, 4096], P('dp', 'seq')
- grad_att_keys: bfloat16 [4, 4096, 4096], P('dp', 'seq')
- grad_receptance: bfloat16 [4, 4096, 4096], P('dp', 'seq')
- grad_mix_keys: bfloat16 [4, 4096, 4096], P('dp', 'seq')
- grad_mix_values: bfloat16 [4, 4096, 4096], P('dp', 'seq')
- fading_exponent_adjoint: float32 [32, 128], replicated
- diagonal_reward_adjoint: float32 [32, 128], replicated
Inputs may be any that keep to these rules, and one draw needn't show every extreme that they name: `spike_fading_exponent`: zero at most positions.
All inputs are finite; a program needn't handle non-finite values.
Results may differ from a plain program's by a relative error of at most 0.0056.
Values may be sent and summed in bfloat16 or wider, within the bound.
No kernel may reach another device: no remote copies, remote signals or barrier semaphores. Data moves between devices by JAX's collectives and lax.ppermute only.
A program may use at most 192 MiB of HBM per device.

v0:
```python
import functools
import math

import jax
import jax.numpy as jnp
from jax import lax
from jax.sharding import Mesh
from jax.sharding import PartitionSpec as P

WINDOW = 512
SEQ = ("seq_0", "seq_1", "seq_2")
SEQ_DP = ("seq_0", "seq_1", "seq_2", "dp_0", "dp_1")
DP = ("dp_0", "dp_1")


PRECISE = lax.Precision.HIGHEST
EPSILON = 1e-05


def neutral_like(array, identity):
    return jax.tree.map(
        lambda part, zero: jnp.zeros_like(part) + jnp.asarray(zero, part.dtype), array, identity
    )


def entering(array, axes, combine, identity, reverse):
    before = start = neutral_like(array, identity)
    subtotal = array
    for axis in reversed(axes):
        length, here = (lax.axis_size(axis), lax.axis_index(axis))
        pieces = jax.tree.map(lambda part: lax.all_gather(part, axis), subtotal)
        inside, subtotal = (start, start)
        for k in reversed(range(length)) if reverse else range(length):
            passed = k > here if reverse else k < here
            subtotal = combine(subtotal, jax.tree.map(lambda part: part[k], pieces))
            inside = jax.tree.map(lambda new, old: jnp.where(passed, new, old), subtotal, inside)
        before = combine(inside, before)
    return before


def shifted(value, axis, steps):
    count = lax.axis_size(axis)
    leading, last = (max(0, -steps), min(count, count - steps))
    return lax.ppermute(value, axis, [(source, source + steps) for source in range(leading, last)])


def by_axis(array, axes):
    return functools.reduce(lax.psum, axes, array)


def recurrence_tile(
    acceptance_matrix,
    lookup_tile_matrix,
    payload_matrix,
    fading_exponent,
    diagonal_reward_factor_arg,
    memory_arg,
):
    sequence_length = acceptance_matrix.shape[0]
    cumulative = jnp.cumsum(fading_exponent, axis=0)
    before = cumulative - fading_exponent
    attenuated_memory = acceptance_matrix * jnp.exp(before)
    key_scaled = lookup_tile_matrix * jnp.exp(-cumulative)
    scores = jnp.einsum("thi,shi->hts", attenuated_memory, key_scaled, precision=PRECISE)
    row_ids = lax.broadcasted_iota(jnp.int32, (sequence_length, sequence_length), 0)
    col_ids = lax.broadcasted_iota(jnp.int32, (sequence_length, sequence_length), 1)
    scores = jnp.where((col_ids < row_ids)[None], scores, 0.0)
    within_tile_summand = jnp.einsum("hts,shj->thj", scores, payload_matrix, precision=PRECISE)
    between_tiles_summand = jnp.einsum(
        "thi,hij->thj", attenuated_memory, memory_arg, precision=PRECISE
    )
    diagonal_reward_summand = (
        jnp.sum(
            acceptance_matrix * diagonal_reward_factor_arg[None] * lookup_tile_matrix,
            axis=2,
            keepdims=True,
        )
        * payload_matrix
    )
    total_decay = cumulative[-1]
    keys_end = lookup_tile_matrix * jnp.exp(total_decay[None] - cumulative)
    memory_result = jnp.exp(total_decay)[:, :, None] * memory_arg + jnp.einsum(
        "thi,thj->hij", keys_end, payload_matrix, precision=PRECISE
    )
    return (
        between_tiles_summand + within_tile_summand + diagonal_reward_summand,
        memory_result,
        attenuated_memory,
    )


def head_norm(module_result):
    average = jnp.mean(module_result, axis=-1, keepdims=True)
    centered = module_result - average
    variance = jnp.mean(centered * centered, axis=-1, keepdims=True)
    return centered * lax.rsqrt(variance + EPSILON)


def window_mask(sequence_length, reach, first_block):
    width = (reach + 1) * sequence_length
    row_ids = lax.broadcasted_iota(jnp.int32, (sequence_length, width), 0)
    col_ids = lax.broadcasted_iota(jnp.int32, (sequence_length, width), 1)
    return (
        (col_ids > row_ids)
        & (col_ids <= row_ids + reach * sequence_length)
        & (col_ids // sequence_length >= first_block)
    )


def chain_forward(earlier, latter):
    return (earlier[0] * latter[0], latter[0][:, :, None] * earlier[1] + latter[1])


def chain_backward(earlier, latter):
    return (earlier[0] * latter[0], latter[1] + latter[0][:, :, None] * earlier[1])


def local(
    probe_matrix,
    softmax_lookup_matrix,
    acceptance_gate,
    recurrent_lookup_matrix,
    recurrent_payload_matrix,
    upstream_adjoint,
    feature_fading_exponent,
    diagonal_reward_factor,
    spike_fading_exponent,
):
    sequence_length = probe_matrix.shape[1]
    head_total, head_size = feature_fading_exponent.shape
    shape_heads = (sequence_length, head_total, head_size)
    reach = WINDOW // sequence_length
    gsize = math.gcd(head_total, 8)
    groups = head_total // gsize
    acceptance_matrix = acceptance_gate.reshape(shape_heads).astype(jnp.float32)
    lookup_tile_matrix = recurrent_lookup_matrix.reshape(shape_heads).astype(jnp.float32)
    payload_matrix = recurrent_payload_matrix.reshape(shape_heads).astype(jnp.float32)
    surge_values = spike_fading_exponent.reshape(sequence_length, head_total)
    fading_exponent = surge_values[:, :, None] - jnp.exp(feature_fading_exponent)[None]
    cumulative = jnp.cumsum(fading_exponent, axis=0)
    total_decay = cumulative[-1]
    fade_all = jnp.exp(total_decay)
    summary = jnp.einsum(
        "thi,thj->hij",
        lookup_tile_matrix * jnp.exp(total_decay[None] - cumulative),
        payload_matrix,
        precision=PRECISE,
    )
    identity = (jnp.ones_like(fade_all), jnp.zeros_like(summary))
    memory_arg = entering((fade_all, summary), SEQ, chain_forward, identity, False)[1]

    def windowed_recurrence(
        acceptance_arg, lookup_arg, payload_arg, fading_exponent_arg, diagonal_reward_factor_arg
    ):
        fading_tile_entries = surge_values[:, :, None] - jnp.exp(fading_exponent_arg)[None]
        module_result, memory_result, attenuated_memory = recurrence_tile(
            acceptance_arg,
            lookup_arg,
            payload_arg,
            fading_tile_entries,
            diagonal_reward_factor_arg,
            memory_arg,
        )
        return ((module_result, memory_result), attenuated_memory)

    (module_result, memory_result), recurrence_adjoint_map, attenuated_memory = jax.vjp(
        windowed_recurrence,
        acceptance_matrix,
        lookup_tile_matrix,
        payload_matrix,
        feature_fading_exponent,
        diagonal_reward_factor,
        has_aux=True,
    )
    normed, norm_pull = jax.vjp(head_norm, module_result)
    blended_tile_entries = normed.astype(jnp.bfloat16)
    query_rows = probe_matrix.reshape(shape_heads)
    akey_rows = softmax_lookup_matrix.reshape(shape_heads)
    cot_rows = upstream_adjoint.reshape(shape_heads)
    earlier = []
    for block in range(reach):
        earlier.append(shifted((akey_rows, blended_tile_entries), SEQ, reach - block))
    keys_all = jnp.concatenate([pair[0] for pair in earlier] + [akey_rows], axis=0)
    values_all = jnp.concatenate([pair[1] for pair in earlier] + [blended_tile_entries], axis=0)
    index = lax.axis_index(SEQ)
    mask = window_mask(sequence_length, reach, reach - index)
    inv_root = head_size ** (-0.5)
    split = reach * sequence_length

    def group_grads(group):
        start = group * gsize
        query_g = lax.dynamic_slice_in_dim(query_rows, start, gsize, 1)
        keys_g = lax.dynamic_slice_in_dim(keys_all, start, gsize, 1)
        values_g = lax.dynamic_slice_in_dim(values_all, start, gsize, 1)
        cot_g = lax.dynamic_slice_in_dim(cot_rows, start, gsize, 1)
        scores = (
            jnp.einsum("lhe,mhe->hlm", query_g, keys_g, preferred_element_type=jnp.float32)
            * inv_root
        )
        scores = jnp.where(mask[None], scores, -1e30)
        highest = jnp.max(scores, axis=2, keepdims=True)
        raised = jnp.exp(scores - highest)
        summed = jnp.sum(raised, axis=2, keepdims=True)
        probabilities = raised / summed
        weights = probabilities.astype(jnp.bfloat16)
        grad_weights = jnp.einsum(
            "lhe,mhe->hlm", cot_g, values_g, preferred_element_type=jnp.float32
        )
        delta_rows = jnp.sum(probabilities * grad_weights, axis=2, keepdims=True)
        grad_scores = probabilities * (grad_weights - delta_rows) * inv_root
        probe_adjoint = jnp.einsum(
            "hlm,mhe->lhe", grad_scores, keys_g.astype(jnp.float32), precision=PRECISE
        )
        query_float = query_g.astype(jnp.float32)
        grad_keys = jnp.einsum(
            "hlm,lhe->mhe", grad_scores[:, :, split:], query_float, precision=PRECISE
        )
        grad_values = jnp.einsum(
            "hlm,lhe->mhe", weights[:, :, split:], cot_g, preferred_element_type=jnp.float32
        )
        return (
            probe_adjoint,
            grad_keys,
            grad_values,
            (highest + jnp.log(summed))[:, :, 0],
            delta_rows[:, :, 0],
        )

    def merge_heads(stacked):
        return jnp.moveaxis(stacked, 0, 1).reshape((stacked.shape[1], head_total, head_size))

    results = lax.map(group_grads, jnp.arange(groups, dtype=jnp.int32))
    probe_adjoint = merge_heads(results[0])
    softmax_lookup_adjoint = merge_heads(results[1])
    blended_adjoint = cot_rows.astype(jnp.float32) + merge_heads(results[2])
    log_totals = results[3].reshape(head_total, sequence_length)
    deltas = results[4].reshape(head_total, sequence_length)
    row_ids = lax.broadcasted_iota(jnp.int32, (sequence_length, sequence_length), 0)
    col_ids = lax.broadcasted_iota(jnp.int32, (sequence_length, sequence_length), 1)
    for ahead in range(1, reach + 1):
        query_next, cot_next = shifted((query_rows, cot_rows), SEQ, -ahead)
        totals_next, delta_next = shifted((log_totals, deltas), SEQ, -ahead)
        valid = (col_ids > row_ids) | (ahead < reach)

        def cross_grads(
            group,
            query_next=query_next,
            cot_next=cot_next,
            totals_next=totals_next,
            delta_next=delta_next,
            valid=valid,
        ):
            start = group * gsize
            query_g = lax.dynamic_slice_in_dim(query_next, start, gsize, 1)
            cot_g = lax.dynamic_slice_in_dim(cot_next, start, gsize, 1)
            keys_g = lax.dynamic_slice_in_dim(akey_rows, start, gsize, 1)
            mixed_g = lax.dynamic_slice_in_dim(blended_tile_entries, start, gsize, 1)
            totals_g = lax.dynamic_slice_in_dim(totals_next, start, gsize, 0)
            delta_g = lax.dynamic_slice_in_dim(delta_next, start, gsize, 0)
            cross_scores = (
                jnp.einsum("lhe,mhe->hlm", query_g, keys_g, preferred_element_type=jnp.float32)
                * inv_root
            )
            cross_scores = jnp.where(valid[None], cross_scores - totals_g[:, :, None], -1e30)
            cross_probs = jnp.exp(cross_scores)
            cross_weights = cross_probs.astype(jnp.bfloat16)
            cross_grad = jnp.einsum(
                "lhe,mhe->hlm", cot_g, mixed_g, preferred_element_type=jnp.float32
            )
            cross_grad = cross_probs * (cross_grad - delta_g[:, :, None]) * inv_root
            part_keys = jnp.einsum(
                "hlm,lhe->mhe", cross_grad, query_g.astype(jnp.float32), precision=PRECISE
            )
            part_values = jnp.einsum(
                "hlm,lhe->mhe", cross_weights, cot_g, preferred_element_type=jnp.float32
            )
            return (part_keys.astype(jnp.bfloat16), part_values.astype(jnp.bfloat16))

        crossed = lax.map(cross_grads, jnp.arange(groups, dtype=jnp.int32))
        softmax_lookup_adjoint = softmax_lookup_adjoint + lax.optimization_barrier(
            merge_heads(crossed[0])
        ).astype(jnp.float32)
        blended_adjoint = blended_adjoint + lax.optimization_barrier(
            merge_heads(crossed[1])
        ).astype(jnp.float32)
    grad_output = norm_pull(blended_adjoint)[0]
    local_grad = jnp.einsum("thi,thj->hij", attenuated_memory, grad_output, precision=PRECISE)
    state_grad = entering((fade_all, local_grad), SEQ, chain_backward, identity, True)[1]
    (
        acceptance_adjoint,
        recurrent_lookup_adjoint,
        recurrent_payload_adjoint,
        fading_exponent_adjoint,
        diagonal_reward_adjoint,
    ) = recurrence_adjoint_map((grad_output, state_grad))
    fading_exponent_adjoint, diagonal_reward_adjoint = (
        by_axis(fading_exponent_adjoint, SEQ_DP),
        by_axis(diagonal_reward_adjoint, SEQ_DP),
    )
    normalizing_denominator = (lax.axis_size(SEQ) * lax.axis_size(DP) * sequence_length) ** (-0.5)
    flat_shape = (1, sequence_length, head_total * head_size)
    return (
        probe_adjoint.reshape(flat_shape).astype(jnp.bfloat16),
        softmax_lookup_adjoint.reshape(flat_shape).astype(jnp.bfloat16),
        acceptance_adjoint.reshape(flat_shape).astype(jnp.bfloat16),
        recurrent_lookup_adjoint.reshape(flat_shape).astype(jnp.bfloat16),
        recurrent_payload_adjoint.reshape(flat_shape).astype(jnp.bfloat16),
        fading_exponent_adjoint * normalizing_denominator,
        diagonal_reward_adjoint * normalizing_denominator,
    )


def solution(mesh):
    finer = Mesh(mesh.devices.reshape(4, 2, 4, 2, 2), ("seq_0", "seq_1", "seq_2", "dp_0", "dp_1"))
    return jax.shard_map(
        local,
        mesh=finer,
        in_specs=(
            P(DP, SEQ, None),
            P(DP, SEQ, None),
            P(DP, SEQ, None),
            P(DP, SEQ, None),
            P(DP, SEQ, None),
            P(DP, SEQ, None),
            P(),
            P(),
            P(DP, SEQ, None),
        ),
        out_specs=(
            P(DP, SEQ, None),
            P(DP, SEQ, None),
            P(DP, SEQ, None),
            P(DP, SEQ, None),
            P(DP, SEQ, None),
            P(),
            P(),
        ),
        check_vma=False,
    )
```

profile of v0, /device:TPU:1, one launch (start us, length us, event | category | flops | bytes accessed | tf_op | source)
XLA Modules:
  0.0 1127.5 jit_solution(1784377697924223996)
XLA Ops:
  25.4 10.4 all_gather.50
  39.2 72.4 %all-gather.17.cloned.1.call-done = f32[128,128,128]{2,1,0:T(8,128)} async-done(((f32[32,128,128]{2,1,0:T(8,128)}), f32[128,128,128]{2,1,0:T(8,128)}) %all-gather.17.cloned.1.call-update) | async-done | bytes 8388624 | tf_op jit(solution)/shard_map/all_gather | solution.py:31
  121.2 57.1 %all-gather.9.cloned.1.call-done = f32[2,32,128,128]{3,2,1,0:T(8,128)} async-done(((f32[1,32,128,128]{3,2,1,0:T(8,128)}), f32[2,32,128,128]{3,2,1,0:T(8,128)}) %all-gather.9.cloned.1.call-update) | async-done | bytes 4194320 | tf_op jit(solution)/shard_map/all_gather | solution.py:31
  208.7 11.0 all_gather.52
  226.1 40.7 %all-gather.11.cloned.1.call-done = f32[4,32,128,128]{3,2,1,0:T(8,128)} async-done(((f32[1,32,128,128]{3,2,1,0:T(8,128)}), f32[4,32,128,128]{3,2,1,0:T(8,128)}) %all-gather.11.cloned.1.call-update) | async-done | bytes 8388624 | tf_op jit(solution)/shard_map/all_gather | solution.py:31
  266.8 9.9 fusion.121
  284.6 16.1 %collective-permute-start.4 = (bf16[128,32,128]{0,2,1:T(8,128)(2,1)}, bf16[128,32,128]{0,2,1:T(8,128)(2,1)}, u32[]{:S(2)}, u32[]{:S(2)}) collective-permute-start(bf16[128,32,128]{0,2,1:T(8,128)(2,1)} %multiply_convert_fusion), channel_id=1, source_target_pairs={{0,16},{4,20},{8,24},{12,28},{16,32},{20,36},{24,40},{28,44},{32,4... | collective-permute-start | bytes 3145736 | tf_op jit(solution)/shard_map/ppermute | solution.py:44
  305.2 90.1 %collective-permute-start.5 = (bf16[128,32,128]{0,2,1:T(8,128)(2,1)}, bf16[128,32,128]{0,2,1:T(8,128)(2,1)S(1)}, u32[]{:S(2)}, u32[]{:S(2)}) collective-permute-start(bf16[128,32,128]{0,2,1:T(8,128)(2,1)} %multiply_convert_fusion), channel_id=1, source_target_pairs={{0,12},{4,16},{8,20},{12,24},{16,28},{20,32},{24,36},{28,40},{32,4... | collective-permute-start | bytes 3145736 | tf_op jit(solution)/shard_map/ppermute | solution.py:44
  416.0 67.6 %collective-permute-done.5 = bf16[128,32,128]{0,2,1:T(8,128)(2,1)S(1)} collective-permute-done((bf16[128,32,128]{0,2,1:T(8,128)(2,1)}, bf16[128,32,128]{0,2,1:T(8,128)(2,1)S(1)}, u32[]{:S(2)}, u32[]{:S(2)}) %collective-permute-start.5) | collective-permute-done | bytes 1048608 | tf_op jit(solution)/shard_map/ppermute | solution.py:44
  487.3 61.2 %while.71 = (s32[]{:T(128)}, bf16[4,128,8,128]{1,3,2,0:T(8,128)(2,1)}, f32[4,128,8,128]{1,3,2,0:T(8,128)}, f32[4,128,8,128]{1,3,2,0:T(8,128)}, f32[4,8,128]{2,1,...) while((s32[]{:T(128)}, ...), condition=%wide.region_8.9_spmd.clone, body=%wide.region_4.8_spmd.clone.sunk | while | flops 1588033536 | bytes 39708604 | solution.py:232
  564.6 31.8 %while.68 = (s32[]{:T(128)}, bf16[4,128,8,128]{1,3,2,0:T(8,128)(2,1)}, bf16[4,128,8,128]{1,3,2,0:T(8,128)(2,1)}, s32[4]{0:T(128)S(1)}, bf16[128,32,128]{0,2,1:T(...) while((s32[]{:T(128)}, ...), condition=%wide.region_10.11_spmd, body=%wide.region_9.10_spmd.sunk | while | flops 303038464 | bytes 4746443 | solution.py:279
  597.7 21.6 %collective-permute-done.12 = bf16[128,32,128]{0,2,1:T(8,128)(2,1)} collective-permute-done((bf16[128,32,128]{0,2,1:T(8,128)(2,1)}, bf16[128,32,128]{0,2,1:T(8,128)(2,1)}, u32[]{:S(2)}, u32[]{:S(2)}) %collective-permute-start.12) | collective-permute-done | bytes 1048608 | tf_op jit(solution)/shard_map/ppermute | solution.py:44
  625.7 31.8 %while.69 = (s32[]{:T(128)}, bf16[4,128,8,128]{1,3,2,0:T(8,128)(2,1)}, bf16[4,128,8,128]{1,3,2,0:T(8,128)(2,1)}, s32[4]{0:T(128)S(1)}, bf16[128,32,128]{0,2,1:T(...) while((s32[]{:T(128)}, ...), condition=%wide.region_12.13_spmd, body=%wide.region_11.12_spmd.sunk | while | flops 303038464 | bytes 4746443 | solution.py:279
  664.2 32.1 %while.70 = (s32[]{:T(128)}, bf16[4,128,8,128]{1,3,2,0:T(8,128)(2,1)}, bf16[4,128,8,128]{1,3,2,0:T(8,128)(2,1)}, s32[4]{0:T(128)S(1)}, bf16[128,32,128]{0,2,1:T(...) while((s32[]{:T(128)}, ...), condition=%wide.region_14.15_spmd, body=%wide.region_13.14_spmd.sunk | while | flops 303038464 | bytes 4746443 | solution.py:279
  698.8 31.3 %while.72 = (s32[]{:T(128)}, bf16[4,128,8,128]{1,3,2,0:T(8,128)(2,1)}, bf16[4,128,8,128]{1,3,2,0:T(8,128)(2,1)}, s32[4]{0:T(128)S(1)}, bf16[128,32,128]{0,2,1:T(...) while((s32[]{:T(128)}, ...), condition=%wide.region_16.17_spmd.clone, body=%wide.region_15.16_spmd.clone.sunk | while | flops 303185920 | bytes 4779211 | solution.py:279
  743.1 116.3 %all-gather.19.cloned.1.call-done = f32[128,128,128]{2,1,0:T(8,128)} async-done(((f32[32,128,128]{2,1,0:T(8,128)}), f32[128,128,128]{2,1,0:T(8,128)}) %all-gather.19.cloned.1.call-update) | async-done | bytes 8388624 | tf_op jit(solution)/shard_map/all_gather | solution.py:31
  865.7 60.3 %all-gather.13.cloned.1.call-done = f32[2,32,128,128]{3,2,1,0:T(8,128)} async-done(((f32[1,32,128,128]{3,2,1,0:T(8,128)}), f32[2,32,128,128]{3,2,1,0:T(8,128)}) %all-gather.13.cloned.1.call-update) | async-done | bytes 4194320 | tf_op jit(solution)/shard_map/all_gather | solution.py:31
  929.8 9.6 all_gather.62
  999.5 14.4 %all-gather.15.cloned.1.call-done = f32[4,32,128,128]{3,2,1,0:T(8,128)} async-done(((f32[1,32,128,128]{3,2,1,0:T(8,128)}), f32[4,32,128,128]{3,2,1,0:T(8,128)}) %all-gather.15.cloned.1.call-update) | async-done | bytes 8388624 | tf_op jit(solution)/shard_map/all_gather | solution.py:31
  1014.0 11.3 %multiply_reduce_fusion.1 = (f32[32,128]{1,0:T(8,128)S(1)}, f32[32,128,128]{2,1,0:T(8,128)S(1)}) fusion(f32[32,128,128]{2,1,0:T(8,128)} %copy-done.7, pred[]{:T(512)S(6)} %lt.102, pred[]{:T(512)S(6)} %lt.101, pred[]{:T(512)S(6)} %lt.100, f32[32,128]{1,0:T(8,128)S(1)} %get-tuple-element.1158, f32[4,32,128,128]{3,2,1,0:T(8,128)} %all-gather.15.cloned.1.call-done, ...), kind=kLoop, calls=%fused_computation.238 | loop fusion | flops 17297408 | bytes 25378826 | tf_op jit(solution)/shard_map/transpose(jvp())/reduce_sum | solution.py:82
  1051.6 12.0 %all-reduce.2 = (f32[32,128]{1,0:T(8,128)S(1)}, f32[32,128]{1,0:T(8,128)S(1)}) all-reduce(f32[32,128]{1,0:T(8,128)S(1)} %negate_multiply_fusion, f32[32,128]{1,0:T(8,128)S(1)} %bitcast.503), channel_id=1, replica_groups=mesh['seq_0'=4,'seq_1'=2,'seq_2'=4,'dp_0'=2,'dp_1'=2] {'seq_0'}, use_global_device_ids=true, to_apply=%region_24.25 | all-reduce | flops 8192 | bytes 65536 | tf_op jit(solution)/shard_map/psum | solution.py:48
  1070.5 13.3 %all-reduce.1 = (f32[32,128]{1,0:T(8,128)S(1)}, f32[32,128]{1,0:T(8,128)S(1)}) all-reduce(f32[32,128]{1,0:T(8,128)S(1)} %get-tuple-element.1114, f32[32,128]{1,0:T(8,128)S(1)} %get-tuple-element.1115), channel_id=1, replica_groups=mesh['seq_0'=4,'seq_1'=2,'seq_2'=4,'dp_0'=2,'dp_1'=2] {'seq_2'}, use_global_device_ids=true, to_apply=%region_26.27 | all-reduce | flops 8192 | bytes 65536 | tf_op jit(solution)/shard_map/psum | solution.py:48
  1083.8 9.2 all-reduce.4
  1093.0 15.4 %all-reduce.3 = (f32[32,128]{1,0:T(8,128)S(1)}, f32[32,128]{1,0:T(8,128)S(1)}) all-reduce(f32[32,128]{1,0:T(8,128)S(1)} %get-tuple-element.1112, f32[32,128]{1,0:T(8,128)S(1)} %get-tuple-element.1113), channel_id=1, replica_groups=mesh['seq_0'=4,'seq_1'=2,'seq_2'=4,'dp_0'=2,'dp_1'=2] {'dp_1'}, use_global_device_ids=true, to_apply=%region_28.29 | all-reduce | flops 8192 | bytes 65536 | tf_op jit(solution)/shard_map/psum | solution.py:48
  (381 shorter events, 440.1 us)
Async XLA Ops:
  7.2 104.5 %all-gather.17.cloned.1.call-start = ((), (), s32[]{:S(2)}) async-start(), calls=%async_computation.4 | async-start | bytes 10485760 | tf_op jit(solution)/shard_map/all_gather | solution.py:31
  25.4 152.9 %all-gather.9.cloned.1.call-start = ((), (), s32[]{:S(2)}) async-start(), calls=%async_computation | async-start | bytes 6291456 | tf_op jit(solution)/shard_map/all_gather | solution.py:31
  117.9 148.9 %all-gather.11.cloned.1.call-start = ((), (), s32[]{:S(2)}) async-start(), calls=%async_computation.1 | async-start | bytes 10485760 | tf_op jit(solution)/shard_map/all_gather | solution.py:31
  182.1 677.3 %all-gather.19.cloned.1.call-start = ((), (), s32[]{:S(2)}) async-start(), calls=%async_computation.5 | async-start | bytes 10485760 | tf_op jit(solution)/shard_map/all_gather | solution.py:31
  184.6 120.7 %collective-permute-start = (bf16[128,32,128]{0,2,1:T(8,128)(2,1)}, bf16[128,32,128]{0,2,1:T(8,128)(2,1)}, u32[]{:S(2)}, u32[]{:S(2)}) collective-permute-start(bf16[128,32,128]{0,2,1:T(8,128)(2,1)} %bitcast.15), channel_id=1, source_target_pairs={{0,16},{4,20},{8,24},{12,28},{16,32},{20,36},{24,40},{28,44},{32,4... | collective-permute-start | bytes 3145736 | tf_op jit(solution)/shard_map/ppermute | solution.py:44
  187.3 208.0 %collective-permute-start.1 = (bf16[128,32,128]{0,2,1:T(8,128)(2,1)}, bf16[128,32,128]{0,2,1:T(8,128)(2,1)}, u32[]{:S(2)}, u32[]{:S(2)}) collective-permute-start(bf16[128,32,128]{0,2,1:T(8,128)(2,1)} %bitcast.15), channel_id=1, source_target_pairs={{0,12},{4,16},{8,20},{12,24},{16,28},{20,32},{24,36},{28,40},{32,4... | collective-permute-start | bytes 3145736 | tf_op jit(solution)/shard_map/ppermute | solution.py:44
  193.0 203.7 %collective-permute-start.2 = (bf16[128,32,128]{0,2,1:T(8,128)(2,1)}, bf16[128,32,128]{0,2,1:T(8,128)(2,1)}, u32[]{:S(2)}, u32[]{:S(2)}) collective-permute-start(bf16[128,32,128]{0,2,1:T(8,128)(2,1)} %bitcast.15), channel_id=1, source_target_pairs={{0,8},{4,12},{8,16},{12,20},{16,24},{20,28},{24,32},{28,36},{32,40... | collective-permute-start | bytes 3145736 | tf_op jit(solution)/shard_map/ppermute | solution.py:44
  197.3 209.7 %collective-permute-start.3 = (bf16[128,32,128]{0,2,1:T(8,128)(2,1)}, bf16[128,32,128]{0,2,1:T(8,128)(2,1)}, u32[]{:S(2)}, u32[]{:S(2)}) collective-permute-start(bf16[128,32,128]{0,2,1:T(8,128)(2,1)} %bitcast.15), channel_id=1, source_target_pairs={{0,4},{4,8},{8,12},{12,16},{16,20},{20,24},{24,28},{28,32},{32,36}... | collective-permute-start | bytes 3145736 | tf_op jit(solution)/shard_map/ppermute | solution.py:44
  284.6 128.5 %collective-permute-start.4 = (bf16[128,32,128]{0,2,1:T(8,128)(2,1)}, bf16[128,32,128]{0,2,1:T(8,128)(2,1)}, u32[]{:S(2)}, u32[]{:S(2)}) collective-permute-start(bf16[128,32,128]{0,2,1:T(8,128)(2,1)} %multiply_convert_fusion), channel_id=1, source_target_pairs={{0,16},{4,20},{8,24},{12,28},{16,32},{20,36},{24,40},{28,44},{32,4... | collective-permute-start | bytes 3145736 | tf_op jit(solution)/shard_map/ppermute | solution.py:44
  305.2 178.4 %collective-permute-start.5 = (bf16[128,32,128]{0,2,1:T(8,128)(2,1)}, bf16[128,32,128]{0,2,1:T(8,128)(2,1)S(1)}, u32[]{:S(2)}, u32[]{:S(2)}) collective-permute-start(bf16[128,32,128]{0,2,1:T(8,128)(2,1)} %multiply_convert_fusion), channel_id=1, source_target_pairs={{0,12},{4,16},{8,20},{12,24},{16,28},{20,32},{24,36},{28,40},{32,4... | collective-permute-start | bytes 3145736 | tf_op jit(solution)/shard_map/ppermute | solution.py:44
  395.4 88.5 %collective-permute-start.6 = (bf16[128,32,128]{0,2,1:T(8,128)(2,1)}, bf16[128,32,128]{0,2,1:T(8,128)(2,1)S(1)}, u32[]{:S(2)}, u32[]{:S(2)}) collective-permute-start(bf16[128,32,128]{0,2,1:T(8,128)(2,1)} %multiply_convert_fusion), channel_id=1, source_target_pairs={{0,8},{4,12},{8,16},{12,20},{16,24},{20,28},{24,32},{28,36},{32,40... | collective-permute-start | bytes 3145736 | tf_op jit(solution)/shard_map/ppermute | solution.py:44
  396.7 87.4 %collective-permute-start.7 = (bf16[128,32,128]{0,2,1:T(8,128)(2,1)}, bf16[128,32,128]{0,2,1:T(8,128)(2,1)S(1)}, u32[]{:S(2)}, u32[]{:S(2)}) collective-permute-start(bf16[128,32,128]{0,2,1:T(8,128)(2,1)} %multiply_convert_fusion), channel_id=1, source_target_pairs={{0,4},{4,8},{8,12},{12,16},{16,20},{20,24},{24,28},{28,32},{32,36}... | collective-permute-start | bytes 3145736 | tf_op jit(solution)/shard_map/ppermute | solution.py:44
  407.1 149.9 %collective-permute-start.10 = (bf16[128,32,128]{0,2,1:T(8,128)(2,1)}, bf16[128,32,128]{0,2,1:T(8,128)(2,1)}, u32[]{:S(2)}, u32[]{:S(2)}) collective-permute-start(bf16[128,32,128]{0,2,1:T(8,128)(2,1)} %bitcast.17), channel_id=1, source_target_pairs={{4,0},{8,4},{12,8},{16,12},{20,16},{24,20},{28,24},{32,28},{36,32}... | collective-permute-start | bytes 3145736 | tf_op jit(solution)/shard_map/ppermute | solution.py:44
  413.1 145.1 %collective-permute-start.8 = (bf16[128,32,128]{0,2,1:T(8,128)(2,1)}, bf16[128,32,128]{0,2,1:T(8,128)(2,1)}, u32[]{:S(2)}, u32[]{:S(2)}) collective-permute-start(bf16[128,32,128]{0,2,1:T(8,128)(2,1)} %bitcast.16), channel_id=1, source_target_pairs={{4,0},{8,4},{12,8},{16,12},{20,16},{24,20},{28,24},{32,28},{36,32}... | collective-permute-start | bytes 3145736 | tf_op jit(solution)/shard_map/ppermute | solution.py:44
  551.1 45.3 %collective-permute-start.14 = (bf16[128,32,128]{0,2,1:T(8,128)(2,1)}, bf16[128,32,128]{0,2,1:T(8,128)(2,1)}, u32[]{:S(2)}, u32[]{:S(2)}) collective-permute-start(bf16[128,32,128]{0,2,1:T(8,128)(2,1)} %bitcast.17), channel_id=1, source_target_pairs={{8,0},{12,4},{16,8},{20,12},{24,16},{28,20},{32,24},{36,28},{40,32... | collective-permute-start | bytes 3145736 | tf_op jit(solution)/shard_map/ppermute | solution.py:44
  556.9 62.4 %collective-permute-start.12 = (bf16[128,32,128]{0,2,1:T(8,128)(2,1)}, bf16[128,32,128]{0,2,1:T(8,128)(2,1)}, u32[]{:S(2)}, u32[]{:S(2)}) collective-permute-start(bf16[128,32,128]{0,2,1:T(8,128)(2,1)} %bitcast.16), channel_id=1, source_target_pairs={{8,0},{12,4},{16,8},{20,12},{24,16},{28,20},{32,24},{36,28},{40,32... | collective-permute-start | bytes 3145736 | tf_op jit(solution)/shard_map/ppermute | solution.py:44
  558.2 99.2 %collective-permute-start.18 = (bf16[128,32,128]{0,2,1:T(8,128)(2,1)}, bf16[128,32,128]{0,2,1:T(8,128)(2,1)}, u32[]{:S(2)}, u32[]{:S(2)}) collective-permute-start(bf16[128,32,128]{0,2,1:T(8,128)(2,1)} %bitcast.17), channel_id=1, source_target_pairs={{12,0},{16,4},{20,8},{24,12},{28,16},{32,20},{36,24},{40,28},{44,3... | collective-permute-start | bytes 3145736 | tf_op jit(solution)/shard_map/ppermute | solution.py:44
  559.6 61.0 %collective-permute-start.13 = (f32[32,128]{1,0:T(8,128)S(1)}, f32[32,128]{1,0:T(8,128)S(1)}, u32[]{:S(2)}, u32[]{:S(2)}) collective-permute-start(f32[32,128]{1,0:T(8,128)S(1)} %bitcast.506), channel_id=1, source_target_pairs={{8,0},{12,4},{16,8},{20,12},{24,16},{28,20},{32,24},{36,28},{40,32... | collective-permute-start | bytes 49160 | tf_op jit(solution)/shard_map/ppermute | solution.py:44
  560.9 61.0 %collective-permute-start.15 = (f32[32,128]{1,0:T(8,128)S(1)}, f32[32,128]{1,0:T(8,128)S(1)}, u32[]{:S(2)}, u32[]{:S(2)}) collective-permute-start(f32[32,128]{1,0:T(8,128)S(1)} %bitcast.510), channel_id=1, source_target_pairs={{8,0},{12,4},{16,8},{20,12},{24,16},{28,20},{32,24},{36,28},{40,32... | collective-permute-start | bytes 49160 | tf_op jit(solution)/shard_map/ppermute | solution.py:44
  596.4 62.4 %collective-permute-start.16 = (bf16[128,32,128]{0,2,1:T(8,128)(2,1)}, bf16[128,32,128]{0,2,1:T(8,128)(2,1)}, u32[]{:S(2)}, u32[]{:S(2)}) collective-permute-start(bf16[128,32,128]{0,2,1:T(8,128)(2,1)} %bitcast.16), channel_id=1, source_target_pairs={{12,0},{16,4},{20,8},{24,12},{28,16},{32,20},{36,24},{40,28},{44,3... | collective-permute-start | bytes 3145736 | tf_op jit(solution)/shard_map/ppermute | solution.py:44
  619.3 77.1 %collective-permute-start.22 = (bf16[128,32,128]{0,2,1:T(8,128)(2,1)}, bf16[128,32,128]{0,2,1:T(8,128)(2,1)}, u32[]{:S(2)}, u32[]{:S(2)}) collective-permute-start(bf16[128,32,128]{0,2,1:T(8,128)(2,1)} %bitcast.17), channel_id=1, source_target_pairs={{16,0},{20,4},{24,8},{28,12},{32,16},{36,20},{40,24},{44,28},{48,3... | collective-permute-start | bytes 3145736 | tf_op jit(solution)/shard_map/ppermute | solution.py:44
  621.9 39.9 %collective-permute-start.19 = (f32[32,128]{1,0:T(8,128)S(1)}, f32[32,128]{1,0:T(8,128)S(1)}, u32[]{:S(2)}, u32[]{:S(2)}) collective-permute-start(f32[32,128]{1,0:T(8,128)S(1)} %bitcast.511), channel_id=1, source_target_pairs={{12,0},{16,4},{20,8},{24,12},{28,16},{32,20},{36,24},{40,28},{44,3... | collective-permute-start | bytes 49160 | tf_op jit(solution)/shard_map/ppermute | solution.py:44
  743.0 183.0 %all-gather.13.cloned.1.call-start = ((), (), s32[]{:S(2)}) async-start(), calls=%async_computation.2 | async-start | bytes 6291456 | tf_op jit(solution)/shard_map/all_gather | solution.py:31
  865.6 148.4 %all-gather.15.cloned.1.call-start = ((), (), s32[]{:S(2)}) async-start(), calls=%async_computation.3 | async-start | bytes 10485760 | tf_op jit(solution)/shard_map/all_gather | solution.py:31
  (43 other events, 817.0 us)
Sparse Core Ops, SparseCore 0:
  25.5 86.1 all-gather.16
  118.0 60.2 all-gather.8
  182.2 84.5 all-gather.10
  743.1 116.1 all-gather.18
  865.7 60.2 all-gather.12
  929.9 83.9 all-gather.14
where the time goes:
time: 1140 us; the launch traced here: 1130 us
  waiting for transfers between devices  451 us (40%)
  matrix products  209 us (18%)
  starting transfers between devices  147 us (13%)
  local copies, waits for them, and re-layouts  110 us (10%)
  blocking collectives  94.5 us (8%)
  other arithmetic  87.1 us (8%)
  between operations  15.5 us (1%)
  loops' own time  13.2 us (1%)
    all_gather x6, waiting for transfers between devices, entering(): pieces = jax.tree.map(lambda part: lax.all_gather(part, axis), subtotal)  361 us
    ppermute x24, starting transfers between devices, shifted(): lax.ppermute(value, axis, [(source, source + steps) for source in range(l...  147 us
    ppermute x24, waiting for transfers between devices, shifted(): lax.ppermute(value, axis, [(source, source + steps) for source in range(l...  89.3 us
    psum x5, blocking collectives, by_axis(): return functools.reduce(lax.psum, axes, array)  56.9 us
    all_gather x5, blocking collectives, entering(): pieces = jax.tree.map(lambda part: lax.all_gather(part, axis), subtotal)  37.6 us
    dot_general x16, matrix products, cross_grads(): jnp.einsum('hlm,lhe->mhe', cross_grad, query_g.astype(jnp.float32), preci...  33 us
    unnamed x73, local copies, waits for them, and re-layouts  31.8 us
    dot_general x16, matrix products, cross_grads(): jnp.einsum('hlm,lhe->mhe', cross_weights, cot_g, preferred_element_type=j...  30 us
  transfers between devices with their start and end apart: 30, of which 8 were waited for; matrix products, arithmetic and copies ran while one was open for 24% of the time, Pallas kernels for 0%

commit v1 on v0

v1 whole, which is shorter than its diff:
```python
import functools
import math

import jax
import jax.numpy as jnp
from jax import lax
from jax.experimental import pallas as pl
from jax.experimental.pallas import tpu as pltpu
from jax.sharding import PartitionSpec as P

F32 = jnp.float32
BF16 = jnp.bfloat16
EPSILON = 1e-05
NEG = -1e30
B = 128
REACH = 4
SPIKE_ROWS = 16
NN = (((1,), (0,)), ((), ()))
NT = (((1,), (1,)), ((), ()))
TN = (((0,), (0,)), ((), ()))


def dot(a, b, dims):
    return lax.dot_general(a, b, dims, preferred_element_type=F32)


def split(x):
    high = x.astype(BF16)
    return high, (x - high.astype(F32)).astype(BF16)


def dot_a(a, b, dims):
    return dot(a[0], b, dims) + dot(a[1], b, dims)


def dot_b(a, b, dims):
    return dot(a, b[0], dims) + dot(a, b[1], dims)


def dot3(a, b, dims):
    return dot(a[0], b[0], dims) + dot(a[0], b[1], dims) + dot(a[1], b[0], dims)


def iota(axis, shape=(B, B)):
    return lax.broadcasted_iota(jnp.int32, shape, axis)


def vmem():
    return pl.BlockSpec(memory_space=pltpu.VMEM)


def smem():
    return pl.BlockSpec(memory_space=pltpu.SMEM)


def params(mib=48):
    return pltpu.CompilerParams(vmem_limit_bytes=mib << 20)


def cost(flops, nbytes):
    return pl.CostEstimate(flops=int(flops), bytes_accessed=int(nbytes), transcendentals=0)


def three_parts(pair):
    row = iota(0, (SPIKE_ROWS, B))
    tile = jnp.zeros((SPIKE_ROWS, B), F32)
    for n, rest in enumerate(pair):
        for m in range(3):
            part = rest.astype(BF16).astype(F32)
            rest = rest - part
            tile = jnp.where(row == 3 * n + m, part, tile)
    return tile.astype(BF16)


def pack(arrays, spike, per=16):
    heads = arrays[0].shape[1] // B
    count = len(arrays)
    extra = 0 if spike is None else SPIKE_ROWS
    rows = count * B + extra

    def kernel(*refs):
        out = refs[-2] if extra else refs[-1]
        for j in range(per):
            for a in range(count):
                out[j, a * B : (a + 1) * B, :] = refs[a][:, j * B : (j + 1) * B]
        if extra:
            sums = refs[-1]
            step = pl.program_id(0)

            @pl.when(step == 0)
            def _():
                surge = refs[count][...]
                upto = jnp.where(iota(0) <= iota(1), 1.0, 0.0).astype(F32)
                below = jnp.where(iota(0) < iota(1), 1.0, 0.0).astype(F32)
                for n, mask in enumerate((upto, below)):
                    sums[n] = lax.dot_general(
                        surge, mask, NN, precision=lax.Precision.HIGHEST, preferred_element_type=F32
                    )

            for j in range(per):
                out[j, count * B :, :] = three_parts(
                    [sums[n, pl.ds(step * per + j, 1), :] for n in range(2)]
                )

    specs = [pl.BlockSpec((B, per * B), lambda i: (0, i)) for _ in arrays]
    operands = list(arrays)
    scratch = []
    if extra:
        specs.append(pl.BlockSpec(spike.shape, lambda i: (0, 0)))
        operands.append(spike)
        scratch = [pltpu.VMEM((2, heads, B), F32)]
    return pl.pallas_call(
        kernel,
        grid=(heads // per,),
        in_specs=specs,
        out_specs=pl.BlockSpec((per, rows, B), lambda i: (i, 0, 0)),
        out_shape=jax.ShapeDtypeStruct((heads, rows, B), BF16),
        scratch_shapes=scratch,
        cost_estimate=cost(0, 2 * heads * rows * B * 2),
        name="pack",
    )(*operands)


def unpack(packed, count, per=16):
    heads, rows, _ = packed.shape

    def kernel(x, *outs):
        for a in range(count):
            for j in range(per):
                outs[a][:, j * B : (j + 1) * B] = x[j, a * B : (a + 1) * B, :]

    return pl.pallas_call(
        kernel,
        grid=(heads // per,),
        in_specs=[pl.BlockSpec((per, rows, B), lambda i: (i, 0, 0))],
        out_specs=[pl.BlockSpec((B, per * B), lambda i: (0, i)) for _ in range(count)],
        out_shape=[jax.ShapeDtypeStruct((B, heads * B), BF16) for _ in range(count)],
        cost_estimate=cost(0, 2 * heads * count * B * B * 2),
        name="unpack",
    )(packed)


def decay_tables(rate, tables):
    position = iota(0).astype(F32)
    tables[0] = jnp.exp(-position * rate)
    tables[1] = jnp.exp((position + 1.0) * rate)
    tables[2] = jnp.exp(-(B - 1.0 - position) * rate)


def chunk_terms(x, n, tables, gain):
    base = 3 * B
    acceptance = x[n, 0:B, :].astype(F32)
    lookup = x[n, B : 2 * B, :].astype(F32)
    payload = x[n, 2 * B : 3 * B, :]
    surges = x[n, base : base + SPIKE_ROWS, :].astype(F32)
    upto = surges[0:1] + surges[1:2] + surges[2:3]
    below = surges[3:4] + surges[4:5] + surges[5:6]
    diagonal = iota(0) == iota(1)
    below_col = jnp.sum(jnp.where(diagonal, below, 0.0), axis=1, keepdims=True)
    upto_col = jnp.sum(jnp.where(diagonal, upto, 0.0), axis=1, keepdims=True)
    total = upto[:, B - 1 : B]
    lower = iota(1) < iota(0)
    fade = jnp.where(lower, jnp.exp(below_col - upto), 0.0)
    entered = jnp.exp(below_col)
    leaving = jnp.exp(total - upto_col)
    queries = acceptance * tables[0]
    keys = lookup * tables[1]
    keys_end = lookup * tables[2] * leaving
    bonus = jnp.sum(acceptance * gain * lookup, axis=1, keepdims=True)
    queries_s, keys_s = split(queries), split(keys)
    scores = dot3(queries_s, keys_s, NT) * fade + jnp.where(diagonal, bonus, 0.0)
    return dict(
        acceptance=acceptance,
        lookup=lookup,
        payload=payload,
        fade=fade,
        entered=entered,
        leaving=leaving,
        total=jnp.exp(total),
        queries=queries,
        queries_s=queries_s,
        keys_s=keys_s,
        keys_end=keys_end,
        keys_end_s=split(keys_end),
        scores=scores,
    )


def head_rows(index, fading, gain):
    return jnp.exp(fading[pl.ds(index, 1), :]), gain[pl.ds(index, 1), :]


def mix_forward(received, index, fading, gain, per=8):
    blocks, rows, _ = received.shape

    def kernel(index_ref, x, fading_ref, gain_ref, mixed, module, states, tables, memory):
        rate, gain_row = head_rows(index_ref[0], fading_ref, gain_ref)

        @pl.when(pl.program_id(0) == 0)
        def _():
            decay_tables(rate, tables)
            memory[...] = jnp.zeros_like(memory)

        whole = jnp.exp(-float(B) * rate)
        state = memory[...]
        for n in range(per):
            c = chunk_terms(x, n, tables, gain_row)
            states[n] = state
            out = dot_a(split(c["scores"]), c["payload"], NN) + c["entered"] * dot3(
                c["queries_s"], split(state), NT
            )
            state = state * (whole * c["total"]) + dot_b(c["payload"], c["keys_end_s"], TN)
            module[n] = out
            average = jnp.mean(out, axis=1, keepdims=True)
            centered = out - average
            variance = jnp.mean(centered * centered, axis=1, keepdims=True)
            mixed[n] = (centered * lax.rsqrt(variance + EPSILON)).astype(BF16)
        memory[...] = state

    block = lambda: pl.BlockSpec((per, B, B), lambda i: (i, 0, 0))
    whole_array = lambda a: pl.BlockSpec(a.shape, lambda i: (0, 0))
    return pl.pallas_call(
        kernel,
        grid=(blocks // per,),
        in_specs=[
            smem(),
            pl.BlockSpec((per, rows, B), lambda i: (i, 0, 0)),
            whole_array(fading),
            whole_array(gain),
        ],
        out_specs=[block(), block(), block()],
        out_shape=[
            jax.ShapeDtypeStruct((blocks, B, B), BF16),
            jax.ShapeDtypeStruct((blocks, B, B), F32),
            jax.ShapeDtypeStruct((blocks, B, B), F32),
        ],
        scratch_shapes=[pltpu.VMEM((3, B, B), F32), pltpu.VMEM((B, B), F32)],
        compiler_params=params(),
        cost_estimate=cost(2e10, 8 << 20),
        name="mix_forward",
    )(index, received, fading, gain)


def mix_backward(received, gradient, module, states, index, fading, gain, per=4):
    blocks, rows, _ = received.shape
    steps = blocks // per

    def kernel(
        index_ref, x, g_ref, module_ref, states_ref, fading_ref, gain_ref, out, tables, memory, sums
    ):
        rate, gain_row = head_rows(index_ref[0], fading_ref, gain_ref)

        @pl.when(pl.program_id(0) == 0)
        def _():
            decay_tables(rate, tables)
            memory[...] = jnp.zeros_like(memory)
            sums[...] = jnp.zeros_like(sums)

        whole = jnp.exp(-float(B) * rate)
        position = iota(0).astype(F32)
        distance = jnp.maximum(iota(0) - iota(1) - 1, 0).astype(F32)
        d_state = memory[...]
        d_rate = jnp.zeros((1, B), F32)
        d_gain = jnp.zeros((1, B), F32)
        first = (steps - 1 - pl.program_id(0)) * per
        for n in reversed(range(per)):
            c = chunk_terms(x, n, tables, gain_row)
            value = module_ref[n]
            centered = value - jnp.mean(value, axis=1, keepdims=True)
            variance = jnp.mean(centered * centered, axis=1, keepdims=True)
            scale = lax.rsqrt(variance + EPSILON)
            normed = centered * scale
            g = g_ref[n]
            grad = scale * (
                g
                - jnp.mean(g, axis=1, keepdims=True)
                - normed * jnp.mean(g * normed, axis=1, keepdims=True)
            )
            grad_s = split(grad)
            state = states_ref[n]
            state_s, d_state_s = split(state), split(d_state)
            payload = c["payload"]
            paired = dot_a(grad_s, payload, NT) * c["fade"]
            paired_s = split(paired)
            own = jnp.sum(grad * payload.astype(F32), axis=1, keepdims=True)
            inter = c["entered"] * dot3(grad_s, state_s, NN)
            d_queries = dot3(paired_s, c["keys_s"], NN) + inter
            d_keys = dot3(paired_s, c["queries_s"], TN)
            d_end = dot_b(payload, d_state_s, NN)
            d_payload = dot3(split(c["scores"]), grad_s, TN) + dot3(c["keys_end_s"], d_state_s, NT)
            out[first + n, 0:B, :] = (
                d_queries * tables[0] + own * gain_row * c["lookup"]
            ).astype(BF16)
            out[first + n, B : 2 * B, :] = (
                d_keys * tables[1]
                + d_end * (tables[2] * c["leaving"])
                + own * gain_row * c["acceptance"]
            ).astype(BF16)
            out[first + n, 2 * B : 3 * B, :] = d_payload.astype(BF16)
            d_gain += jnp.sum(own * c["acceptance"] * c["lookup"], axis=0, keepdims=True)
            spread = dot(
                (paired * distance).astype(BF16), c["keys_s"][0], NN
            )
            carried = whole * c["total"]
            d_rate += jnp.sum(
                c["queries"] * (spread + position * inter)
                + (B - 1.0 - position) * c["keys_end"] * d_end
                + (float(B) * carried) * state * d_state,
                axis=0,
                keepdims=True,
            )
            d_state = d_state * carried + dot3(
                split(grad * c["entered"]), c["queries_s"], TN
            )
        memory[...] = d_state
        sums[0:1, :] += -rate * d_rate
        sums[1:2, :] += d_gain

        @pl.when(pl.program_id(0) == steps - 1)
        def _():
            tile = three_parts([sums[0:1, :], sums[1:2, :]])
            for b in range(blocks):
                out[b, 3 * B :, :] = tile

    back = lambda i: (steps - 1 - i, 0, 0)
    block = lambda: pl.BlockSpec((per, B, B), back)
    whole_array = lambda a: pl.BlockSpec(a.shape, lambda i: (0, 0))
    return pl.pallas_call(
        kernel,
        grid=(steps,),
        in_specs=[
            smem(),
            pl.BlockSpec((per, rows, B), back),
            block(),
            block(),
            block(),
            whole_array(fading),
            whole_array(gain),
        ],
        out_specs=vmem(),
        out_shape=jax.ShapeDtypeStruct((blocks, rows, B), BF16),
        scratch_shapes=[
            pltpu.VMEM((3, B, B), F32),
            pltpu.VMEM((B, B), F32),
            pltpu.VMEM((8, B), F32),
        ],
        compiler_params=params(),
        cost_estimate=cost(2e10, 12 << 20),
        name="mix_backward",
    )(index, received, gradient, module, states, fading, gain)


def attention_grads(received, mixed):
    blocks = received.shape[0]
    pad = REACH * B
    length = blocks * B
    two = 2 * B
    span = pad + two
    inv_root = B ** (-0.5)
    to_log2 = inv_root * math.log2(math.e)

    def kernel(x, m_ref, out, gm, kpad, mpad, dk, dm, s_t, dp_t, w_t, ds_t):
        kpad[0:pad, :] = jnp.zeros((pad, B), BF16)
        mpad[0:pad, :] = jnp.zeros((pad, B), BF16)
        dk[...] = jnp.zeros_like(dk)
        dm[...] = jnp.zeros_like(dm)
        for ref in (w_t, ds_t):
            ref[pad + B :, 0:B] = jnp.zeros((B, B), BF16)
            ref[0:B, B:] = jnp.zeros((B, B), BF16)

        def fill(b, _):
            at = pl.ds(pl.multiple_of(pad + b * B, B), B)
            kpad[at, :] = x[b, B : 2 * B, :]
            mpad[at, :] = m_ref[b]
            return 0

        lax.fori_loop(0, blocks, fill, 0)
        early = iota(0) > iota(1)
        causal = iota(0) <= iota(1)

        def step(i, _, first=None):
            rows = pl.ds(pl.multiple_of(i * two, two), span)
            queries = jnp.concatenate([x[2 * i, 0:B, :], x[2 * i + 1, 0:B, :]], axis=0)
            cots = jnp.concatenate(
                [x[2 * i, 2 * B : 3 * B, :], x[2 * i + 1, 2 * B : 3 * B, :]], axis=0
            )
            keys = kpad[rows, :]
            s_t[...] = dot(keys, queries, NT)
            dp_t[...] = dot(mpad[rows, :], cots, NT)
            for sub in range(2):
                lanes = slice(sub * B, (sub + 1) * B)
                pick = [slice((sub + j) * B, (sub + j + 1) * B) for j in range(REACH + 1)]
                live = [
                    j
                    for j in range(REACH + 1)
                    if first is None or 2 * first + sub - REACH + j >= 0
                ]
                scores = {}
                for j in live:
                    score = s_t[pick[j], lanes]
                    if j == 0:
                        score = jnp.where(early, score, NEG)
                    if j == REACH:
                        score = jnp.where(causal, score, NEG)
                    scores[j] = score
                highest = functools.reduce(
                    jnp.maximum, [jnp.max(scores[j], axis=0, keepdims=True) for j in live]
                )
                raised = {j: jnp.exp2((scores[j] - highest) * to_log2) for j in live}
                total = sum(jnp.sum(raised[j], axis=0, keepdims=True) for j in live)
                inner = sum(
                    jnp.sum(raised[j] * dp_t[pick[j], lanes], axis=0, keepdims=True) for j in live
                )
                share = 1.0 / total
                delta = inner * share
                for j in range(REACH + 1):
                    if j in live:
                        probability = raised[j] * share
                        w_t[pick[j], lanes] = probability.astype(BF16)
                        ds_t[pick[j], lanes] = (
                            probability * ((dp_t[pick[j], lanes] - delta) * inv_root)
                        ).astype(BF16)
                    else:
                        w_t[pick[j], lanes] = jnp.zeros((B, B), BF16)
                        ds_t[pick[j], lanes] = jnp.zeros((B, B), BF16)
            dk[rows, :] += dot(ds_t[...], queries, NN)
            dm[rows, :] += dot(w_t[...], cots, NN)
            dq = dot(ds_t[...], keys, TN).astype(BF16)
            out[2 * i, 0:B, :] = dq[0:B]
            out[2 * i + 1, 0:B, :] = dq[B:]
            return 0

        for i in range(REACH // 2):
            step(i, 0, first=i)
        lax.fori_loop(REACH // 2, blocks // 2, step, 0)

        def flush(b, _):
            at = pl.ds(pl.multiple_of(pad + b * B, B), B)
            out[b, B : 2 * B, :] = dk[at, :].astype(BF16)
            gm[b] = dm[at, :] + x[b, 2 * B : 3 * B, :].astype(F32)
            return 0

        lax.fori_loop(0, blocks, flush, 0)

    return pl.pallas_call(
        kernel,
        in_specs=[vmem(), vmem()],
        out_specs=[vmem(), vmem()],
        out_shape=[
            jax.ShapeDtypeStruct((blocks, 2 * B, B), BF16),
            jax.ShapeDtypeStruct((blocks, B, B), F32),
        ],
        scratch_shapes=[
            pltpu.VMEM((pad + length, B), BF16),
            pltpu.VMEM((pad + length, B), BF16),
            pltpu.VMEM((pad + length, B), F32),
            pltpu.VMEM((pad + length, B), F32),
            pltpu.VMEM((span, two), F32),
            pltpu.VMEM((span, two), F32),
            pltpu.VMEM((span, two), BF16),
            pltpu.VMEM((span, two), BF16),
        ],
        compiler_params=params(),
        cost_estimate=cost(2e10, 8 << 20),
        name="attention_grads",
    )(received, mixed)


def exchange(blocks):
    return lax.all_to_all(blocks, "seq", 0, 0, tiled=True)


def local(
    probe_matrix,
    softmax_lookup_matrix,
    acceptance_gate,
    recurrent_lookup_matrix,
    recurrent_payload_matrix,
    upstream_adjoint,
    feature_fading_exponent,
    diagonal_reward_factor,
    spike_fading_exponent,
):
    positions = probe_matrix.shape[1] * lax.axis_size("seq") * lax.axis_size("dp")
    here = lax.axis_index("seq")
    index = here.astype(jnp.int32).reshape(1)
    mix_in = exchange(
        pack(
            (acceptance_gate[0], recurrent_lookup_matrix[0], recurrent_payload_matrix[0]),
            spike_fading_exponent[0].T,
        )
    )
    att_in = exchange(
        pack((probe_matrix[0], softmax_lookup_matrix[0], upstream_adjoint[0]), None)
    )
    mixed, module, states = mix_forward(
        mix_in, index, feature_fading_exponent, diagonal_reward_factor
    )
    att_out, gradient = attention_grads(att_in, mixed)
    att_back = exchange(att_out)
    mix_out = mix_backward(
        mix_in, gradient, module, states, index, feature_fading_exponent, diagonal_reward_factor
    )
    mix_out, att_back = lax.optimization_barrier((mix_out, att_back))
    mix_back = exchange(mix_out)
    parts = mix_back[:, 3 * B : 3 * B + 6, :].astype(F32)
    sums = jnp.stack([parts[:, 0] + parts[:, 1] + parts[:, 2], parts[:, 3] + parts[:, 4] + parts[:, 5]])
    group = lax.axis_size("dp")
    around = [
        lax.ppermute(sums, "dp", [(i, (i + k) % group) for i in range(group)])
        for k in range(1, group)
    ]
    adjoints = ((sums + around[1]) + (around[0] + around[2])) * positions ** (-0.5)
    dq, dk = unpack(att_back, 2)
    dr, dmk, dmv = unpack(mix_back, 3)
    return (dq[None], dk[None], dr[None], dmk[None], dmv[None], adjoints[0], adjoints[1])


def solution(mesh):
    rows = P("dp", "seq", None)
    return jax.shard_map(
        local,
        mesh=mesh,
        in_specs=(rows,) * 6 + (P(), P(), rows),
        out_specs=(rows,) * 5 + (P(), P()),
        check_vma=False,
    )
```

time: 1140 us -> 224 us (0.20)
  waiting for transfers between devices: 451 us -> 67.8 us
  matrix products: 209 us -> 0 us
  starting transfers between devices: 147 us -> 31.8 us
  local copies, waits for them, and re-layouts: 110 us -> 4.87 us
  other arithmetic: 87.1 us -> 0.1 us
  Pallas kernels: 0 us -> 69.8 us
  blocking collectives: 94.5 us -> 46.2 us
  between operations: 15.5 us -> 0.76 us
  loops' own time: 13.2 us -> 0 us
    all_gather x6 -> x0, waiting for transfers between devices: 361 us -> none  [entering(): pieces = jax.tree.map(lambda part: lax.all_gather(part, axis), subtotal)]
    dot_general x96 -> x0, matrix products: 209 us -> none  [the longest x16 33 us: cross_grads(): jnp.einsum('hlm,lhe->mhe', cross_grad, query_g.astype(jnp.float32), preci...]
    ppermute x24 -> x3, starting transfers between devices: 147 us -> 7.82 us  [local(): lax.ppermute(sums, 'dp', [(i, (i + k) % group) for i in range(group)])]
    ppermute x24 -> x3, waiting for transfers between devices: 89.3 us -> 0.01 us  [local(): lax.ppermute(sums, 'dp', [(i, (i + k) % group) for i in range(group)])]
    pallas_call x0 -> x7, Pallas kernels: none -> 69.8 us  [the longest x1 25.1 us: mix_backward(): pl.pallas_call(kernel, grid=(steps,), in_specs=[smem(), pl.BlockSpec((per...]
    all_to_all x0 -> x3, waiting for transfers between devices: none -> 67.8 us  [exchange(): return lax.all_to_all(blocks, 'seq', 0, 0, tiled=True)]
    psum x5 -> x0, blocking collectives: 56.9 us -> none  [by_axis(): return functools.reduce(lax.psum, axes, array)]
    all_to_all x0 -> x1, blocking collectives: none -> 46.2 us  [exchange(): return lax.all_to_all(blocks, 'seq', 0, 0, tiled=True)]
  transfers between devices with their start and end apart: 30 -> 6, of which waited for: 8 -> 2; matrix products, arithmetic and copies ran while one was open for 24% -> 0% of each run, Pallas kernels for 0% -> 20%
where the time goes in v1:
time: 224 us; the launch traced here: 221 us
  Pallas kernels  69.8 us (31%)
  waiting for transfers between devices  67.8 us (30%)
  blocking collectives  46.2 us (21%)
  starting transfers between devices  31.8 us (14%)
  local copies, waits for them, and re-layouts  4.87 us (2%)
    all_to_all x3, waiting for transfers between devices, exchange(): return lax.all_to_all(blocks, 'seq', 0, 0, tiled=True)  67.8 us
    all_to_all x1, blocking collectives, exchange(): return lax.all_to_all(blocks, 'seq', 0, 0, tiled=True)  46.2 us
    pallas_call x1, Pallas kernels, mix_backward(): pl.pallas_call(kernel, grid=(steps,), in_specs=[smem(), pl.BlockSpec((per...  25.1 us
    all_to_all x3, starting transfers between devices, exchange(): return lax.all_to_all(blocks, 'seq', 0, 0, tiled=True)  23.9 us
    pallas_call x1, Pallas kernels, attention_grads(): pl.pallas_call(kernel, in_specs=[vmem(), vmem()], out_specs=[vmem(), vmem...  21 us
    pallas_call x1, Pallas kernels, mix_forward(): pl.pallas_call(kernel, grid=(blocks // per,), in_specs=[smem(), pl.BlockS...  10.2 us
    ppermute x3, starting transfers between devices, local(): lax.ppermute(sums, 'dp', [(i, (i + k) % group) for i in range(group)])  7.82 us
    pallas_call x2, Pallas kernels, pack(): pl.pallas_call(kernel, grid=(heads // per,), in_specs=specs, out_specs=pl...  7.12 us
  transfers between devices with their start and end apart: 6, of which 2 were waited for; matrix products, arithmetic and copies ran while one was open for 0% of the time, Pallas kernels for 20%

profile of v1, /device:TPU:1, one launch (start us, length us, event | category | flops | bytes accessed | tf_op | source)
XLA Modules:
  0.0 221.3 jit_solution(10336486503285923142)
XLA Ops:
  0.6 3.7 %pack.2 = bf16[32,400,128]{2,1,0:T(8,128)(2,1)} custom-call(bf16[128,4096]{1,0:T(8,128)(2,1)} %bitcast.25, bf16[128,4096]{1,0:T(8,128)(2,1)} %bitcast.26, bf16[128,4096]{1,0:T(8,128)(2,1)} %bitcast.27, f32[32,128]{1,0:T(8,128)} %bitcast.36), custom_call_target="tpu_custom_call" | custom-call | bytes 6553600 | tf_op jit(solution)/shard_map/pack/pallas_call | solution.py:112
  4.4 9.3 %all-to-all-start = ((bf16[32,400,128]{2,1,0:T(8,128)(2,1)}), bf16[32,400,128]{2,1,0:T(8,128)(2,1)}, u32[]{:S(2)}, u32[]{:S(2)}) async-start(bf16[32,400,128]{2,1,0:T(8,128)(2,1)} %pack.2), calls=%async_computation | async-start | bytes 6553600 | tf_op jit(solution)/shard_map/all_to_all | solution.py:470
  13.7 3.4 %pack.3 = bf16[32,384,128]{2,1,0:T(8,128)(2,1)} custom-call(bf16[128,4096]{1,0:T(8,128)(2,1)} %bitcast.28, bf16[128,4096]{1,0:T(8,128)(2,1)} %bitcast.29, bf16[128,4096]{1,0:T(8,128)(2,1)} %bitcast.30), custom_call_target="tpu_custom_call" | custom-call | bytes 6291456 | tf_op jit(solution)/shard_map/pack/pallas_call | solution.py:112
  17.1 39.0 %all-to-all-done.x = bf16[32,400,128]{2,1,0:T(8,128)(2,1)} async-done(((bf16[32,400,128]{2,1,0:T(8,128)(2,1)}), bf16[32,400,128]{2,1,0:T(8,128)(2,1)}, u32[]{:S(2)}, u32[]{:S(2)}) %all-to-all-start) | async-done | bytes 3276832 | tf_op jit(solution)/shard_map/all_to_all | solution.py:470
  56.1 8.0 %all-to-all-start.1 = ((bf16[32,384,128]{2,1,0:T(8,128)(2,1)}), bf16[32,384,128]{2,1,0:T(8,128)(2,1)}, u32[]{:S(2)}, u32[]{:S(2)}) async-start(bf16[32,384,128]{2,1,0:T(8,128)(2,1)} %pack.3), calls=%async_computation.1 | async-start | bytes 6291456 | tf_op jit(solution)/shard_map/all_to_all | solution.py:470
  64.1 10.2 %mix_forward.1 = (bf16[32,128,128]{2,1,0:T(8,128)(2,1)S(1)}, f32[32,128,128]{2,1,0:T(8,128)S(1)}, f32[32,128,128]{2,1,0:T(8,128)S(1)}) custom-call(s32[1]{0:T(128)} %bitcast.index_ref, bf16[32,400,128]{2,1,0:T(8,128)(2,1)} %all-to-all-done.x, f32[32,128]{1,0:T(8,128)S(1)} %copy-done, f32[32,128]{1,0:T(8,128)S(1)} %copy-done.1), custom_call_target="tpu_custom_call" | custom-call | flops 20000000000 | bytes 8388608 | tf_op jit(solution)/shard_map/mix_forward/pallas_call | solution.py:222
  74.3 1.4 copy-done.2
  75.7 28.8 %all-to-all-done.1.x = bf16[32,384,128]{2,1,0:T(8,128)(2,1)} async-done(((bf16[32,384,128]{2,1,0:T(8,128)(2,1)}), bf16[32,384,128]{2,1,0:T(8,128)(2,1)}, u32[]{:S(2)}, u32[]{:S(2)}) %all-to-all-start.1) | async-done | bytes 3145760 | tf_op jit(solution)/shard_map/all_to_all | solution.py:470
  104.5 21.0 %attention_grads.1 = (bf16[32,256,128]{2,1,0:T(8,128)(2,1)}, f32[32,128,128]{2,1,0:T(8,128)S(1)}) custom-call(bf16[32,384,128]{2,1,0:T(8,128)(2,1)} %all-to-all-done.1.x, bf16[32,128,128]{2,1,0:T(8,128)(2,1)S(1)} %get-tuple-element.19.m_ref), custom_call_target="tpu_custom_call" | custom-call | flops 20000000000 | bytes 8388608 | tf_op jit(solution)/shard_map/attention_grads/pallas_call | solution.py:445
  125.5 1.3 copy-done.3
  126.8 6.6 %all-to-all-start.2 = ((bf16[32,256,128]{2,1,0:T(8,128)(2,1)}), bf16[32,256,128]{2,1,0:T(8,128)(2,1)}, u32[]{:S(2)}, u32[]{:S(2)}) async-start(bf16[32,256,128]{2,1,0:T(8,128)(2,1)} %get-tuple-element.23), calls=%async_computation.2 | async-start | bytes 4194304 | tf_op jit(solution)/shard_map/all_to_all | solution.py:470
  133.5 1.6 copy-done.4
  135.1 25.1 %mix_backward.1 = bf16[32,400,128]{2,1,0:T(8,128)(2,1)} custom-call(s32[1]{0:T(128)} %bitcast.index_ref, bf16[32,400,128]{2,1,0:T(8,128)(2,1)} %all-to-all-done.x, f32[32,128,128]{2,1,0:T(8,128)S(1)} %copy-done.4, f32[32,128,128]{2,1,0:T(8,128)S(1)} %get-tuple-element.21.module_ref, f32[32,128,128]{2,1,0:T(8,128)} %copy-done.2, f32[32,128]{1,0:T(8,128)S(1)} %copy-done, ...), custom_call_target="tpu_custom_call" | custom-call | flops 20000000000 | bytes 12582912 | tf_op jit(solution)/shard_map/mix_backward/pallas_call | solution.py:328
  160.2 0.0 all-to-all-done.2.x
  160.2 46.2 %all_to_all.20.x = bf16[32,400,128]{2,1,0:T(8,128)(2,1)S(1)} all-to-all(bf16[32,400,128]{2,1,0:T(8,128)(2,1)} %mix_backward.1), channel_id=1, replica_groups=mesh['seq'=32,'dp'=4] {'seq'}, dimensions={0} | all-to-all | bytes 6553600 | tf_op jit(solution)/shard_map/all_to_all | solution.py:470
  206.4 0.1 fusion
  206.5 7.6 %collective-permute-start.1 = (f32[2,32,128]{2,1,0:T(8,128)S(1)}, f32[2,32,128]{2,1,0:T(8,128)S(1)}, u32[]{:S(2)}, u32[]{:S(2)}) collective-permute-start(f32[2,32,128]{2,1,0:T(8,128)S(1)} %pad_maximum_fusion), channel_id=1, source_target_pairs={{0,1},{1,2},{2,3},{3,0},{4,5},{5,6},{6,7},{7,4},{8,9},{9,10},{10,1... | collective-permute-start | bytes 98312 | tf_op jit(solution)/shard_map/ppermute | solution.py:510
  214.1 0.0 collective-permute-start.2
  214.1 0.2 collective-permute-start
  214.3 2.8 %unpack.2 = (bf16[128,4096]{1,0:T(8,128)(2,1)}, bf16[128,4096]{1,0:T(8,128)(2,1)}) custom-call(bf16[32,256,128]{2,1,0:T(8,128)(2,1)} %all-to-all-done.2.x), custom_call_target="tpu_custom_call" | custom-call | bytes 4194304 | tf_op jit(solution)/shard_map/unpack/pallas_call | solution.py:132
  217.1 3.5 %unpack.3 = (bf16[128,4096]{1,0:T(8,128)(2,1)}, bf16[128,4096]{1,0:T(8,128)(2,1)}, bf16[128,4096]{1,0:T(8,128)(2,1)}) custom-call(bf16[32,400,128]{2,1,0:T(8,128)(2,1)} %copy-done.5), custom_call_target="tpu_custom_call" | custom-call | bytes 6291456 | tf_op jit(solution)/shard_map/unpack/pallas_call | solution.py:132
  220.6 0.0 collective-permute-done.1
  220.6 0.0 collective-permute-done.2
  220.7 0.6 slice_bitcast_fusion
  (14 shorter events, 0.1 us)
Async XLA Ops:
  4.4 51.7 %all-to-all-start = ((bf16[32,400,128]{2,1,0:T(8,128)(2,1)}), bf16[32,400,128]{2,1,0:T(8,128)(2,1)}, u32[]{:S(2)}, u32[]{:S(2)}) async-start(bf16[32,400,128]{2,1,0:T(8,128)(2,1)} %pack.2), calls=%async_computation | async-start | bytes 6553600 | tf_op jit(solution)/shard_map/all_to_all | solution.py:470
  17.1 47.0 %copy-start = (f32[32,128]{1,0:T(8,128)S(1)}, f32[32,128]{1,0:T(8,128)}, u32[]{:S(2)}) copy-start(f32[32,128]{1,0:T(8,128)} %fading_ref.3) | copy-start | bytes 49156
  17.1 47.0 %copy-start.1 = (f32[32,128]{1,0:T(8,128)S(1)}, f32[32,128]{1,0:T(8,128)}, u32[]{:S(2)}) copy-start(f32[32,128]{1,0:T(8,128)} %gain_ref.3) | copy-start | bytes 49156
  56.1 48.4 %all-to-all-start.1 = ((bf16[32,384,128]{2,1,0:T(8,128)(2,1)}), bf16[32,384,128]{2,1,0:T(8,128)(2,1)}, u32[]{:S(2)}, u32[]{:S(2)}) async-start(bf16[32,384,128]{2,1,0:T(8,128)(2,1)} %pack.3), calls=%async_computation.1 | async-start | bytes 6291456 | tf_op jit(solution)/shard_map/all_to_all | solution.py:470
  74.3 1.4 copy-start.2
  125.5 1.3 copy-start.3
  126.8 33.4 %all-to-all-start.2 = ((bf16[32,256,128]{2,1,0:T(8,128)(2,1)}), bf16[32,256,128]{2,1,0:T(8,128)(2,1)}, u32[]{:S(2)}, u32[]{:S(2)}) async-start(bf16[32,256,128]{2,1,0:T(8,128)(2,1)} %get-tuple-element.23), calls=%async_computation.2 | async-start | bytes 4194304 | tf_op jit(solution)/shard_map/all_to_all | solution.py:470
  133.5 1.6 copy-start.4
  206.4 10.7 %copy-start.5 = (bf16[32,400,128]{2,1,0:T(8,128)(2,1)}, bf16[32,400,128]{2,1,0:T(8,128)(2,1)S(1)}, u32[]{:S(2)}) copy-start(bf16[32,400,128]{2,1,0:T(8,128)(2,1)S(1)} %all_to_all.20.x) | copy-start | bytes 9830404
  206.5 14.1 %collective-permute-start.1 = (f32[2,32,128]{2,1,0:T(8,128)S(1)}, f32[2,32,128]{2,1,0:T(8,128)S(1)}, u32[]{:S(2)}, u32[]{:S(2)}) collective-permute-start(f32[2,32,128]{2,1,0:T(8,128)S(1)} %pad_maximum_fusion), channel_id=1, source_target_pairs={{0,1},{1,2},{2,3},{3,0},{4,5},{5,6},{6,7},{7,4},{8,9},{9,10},{10,1... | collective-permute-start | bytes 98312 | tf_op jit(solution)/shard_map/ppermute | solution.py:510
  214.1 6.5 %collective-permute-start.2 = (f32[2,32,128]{2,1,0:T(8,128)S(1)}, f32[2,32,128]{2,1,0:T(8,128)S(1)}, u32[]{:S(2)}, u32[]{:S(2)}) collective-permute-start(f32[2,32,128]{2,1,0:T(8,128)S(1)} %pad_maximum_fusion), channel_id=1, source_target_pairs={{0,3},{1,0},{2,1},{3,2},{4,7},{5,4},{6,5},{7,6},{8,11},{9,8},{10,9... | collective-permute-start | bytes 98312 | tf_op jit(solution)/shard_map/ppermute | solution.py:510
  214.1 6.5 %collective-permute-start = (f32[2,32,128]{2,1,0:T(8,128)S(1)}, f32[2,32,128]{2,1,0:T(8,128)S(1)}, u32[]{:S(2)}, u32[]{:S(2)}) collective-permute-start(f32[2,32,128]{2,1,0:T(8,128)S(1)} %pad_maximum_fusion), channel_id=1, source_target_pairs={{0,2},{1,3},{2,0},{3,1},{4,6},{5,7},{6,4},{7,5},{8,10},{9,11},{10,... | collective-permute-start | bytes 98312 | tf_op jit(solution)/shard_map/ppermute | solution.py:510

commit v2 on v1

v2 whole, which is shorter than its diff:
```python
import functools
import math

import jax
import jax.numpy as jnp
from jax import lax
from jax.experimental import pallas as pl
from jax.experimental.pallas import tpu as pltpu
from jax.sharding import PartitionSpec as P

F32 = jnp.float32
BF16 = jnp.bfloat16
EPSILON = 1e-05
NEG = -1e30
LOG2E = math.log2(math.e)
B = 128
REACH = 4
SPIKE_ROWS = 16
QUERIES = 3 * B
KEYS = 4 * B
SPIKES = 5 * B
SUMS = 3 * B
PAD = REACH * B
TWO = 2 * B
SPAN = PAD + TWO
INV_ROOT = B ** (-0.5)
NN = (((1,), (0,)), ((), ()))
NT = (((1,), (1,)), ((), ()))
TN = (((0,), (0,)), ((), ()))


def dot(a, b, dims):
    return lax.dot_general(a, b, dims, preferred_element_type=F32)


def split(x):
    high = x.astype(BF16)
    return high, (x - high.astype(F32)).astype(BF16)


def dot_a(a, b, dims):
    return dot(a[0], b, dims) + dot(a[1], b, dims)


def dot_b(a, b, dims):
    return dot(a, b[0], dims) + dot(a, b[1], dims)


def dot3(a, b, dims):
    return dot(a[0], b[0], dims) + dot(a[0], b[1], dims) + dot(a[1], b[0], dims)


def iota(axis, shape=(B, B)):
    return lax.broadcasted_iota(jnp.int32, shape, axis)


def vmem():
    return pl.BlockSpec(memory_space=pltpu.VMEM)


def smem():
    return pl.BlockSpec(memory_space=pltpu.SMEM)


def params(mib=58):
    return pltpu.CompilerParams(vmem_limit_bytes=mib << 20)


def cost(flops, nbytes):
    return pl.CostEstimate(flops=int(flops), bytes_accessed=int(nbytes), transcendentals=0)


def three_parts(pair):
    row = iota(0, (SPIKE_ROWS, B))
    tile = jnp.zeros((SPIKE_ROWS, B), F32)
    for n, rest in enumerate(pair):
        for m in range(3):
            part = rest.astype(BF16).astype(F32)
            rest = rest - part
            tile = jnp.where(row == 3 * n + m, part, tile)
    return tile.astype(BF16)


def pack(arrays, cots, spike, per=8):
    heads = cots.shape[1] // B
    count = len(arrays)
    steps = heads // per
    rows = SPIKES + SPIKE_ROWS

    def kernel(*refs):
        sources, surge_ref = refs[: count + 1], refs[count + 1]
        first, second, first_buf, second_buf, sums, first_sem, second_sem = refs[count + 2 :]
        step = pl.program_id(0)

        def leaving(h):
            return pltpu.make_async_copy(first_buf.at[h], first.at[h], first_sem.at[h])

        def leaving_cots(g):
            at = pl.ds(g * per, per)
            return pltpu.make_async_copy(second_buf.at[at], second.at[at], second_sem.at[g])

        @pl.when(step == 0)
        def _():
            surge = surge_ref[...]
            upto = jnp.where(iota(0) <= iota(1), 1.0, 0.0).astype(F32)
            below = jnp.where(iota(0) < iota(1), 1.0, 0.0).astype(F32)
            for n, mask in enumerate((upto, below)):
                sums[n] = lax.dot_general(
                    surge, mask, NN, precision=lax.Precision.HIGHEST, preferred_element_type=F32
                )

        for j in range(per):
            h = step * per + j
            columns = slice(j * B, (j + 1) * B)
            for a in range(count):
                first_buf[h, a * B : (a + 1) * B, :] = sources[a][:, columns]
            first_buf[h, SPIKES:, :] = three_parts([sums[n, pl.ds(h, 1), :] for n in range(2)])
            leaving(h).start()
            second_buf[h] = sources[count][:, columns]
        leaving_cots(step).start()

        @pl.when(step == steps - 1)
        def _():
            for h in range(heads):
                leaving(h).wait()
            for g in range(steps):
                leaving_cots(g).wait()

    return pl.pallas_call(
        kernel,
        grid=(steps,),
        in_specs=[pl.BlockSpec((B, per * B), lambda i: (0, i)) for _ in range(count + 1)]
        + [pl.BlockSpec(spike.shape, lambda i: (0, 0))],
        out_specs=[pl.BlockSpec(memory_space=pl.ANY)] * 2,
        out_shape=[
            jax.ShapeDtypeStruct((heads, rows, B), BF16),
            jax.ShapeDtypeStruct((heads, B, B), BF16),
        ],
        scratch_shapes=[
            pltpu.VMEM((heads, rows, B), BF16),
            pltpu.VMEM((heads, B, B), BF16),
            pltpu.VMEM((2, heads, B), F32),
            pltpu.SemaphoreType.DMA((heads,)),
            pltpu.SemaphoreType.DMA((steps,)),
        ],
        compiler_params=params(),
        cost_estimate=cost(0, 2 * heads * (rows + B) * B * 2),
        name="pack",
    )(*arrays, cots, spike)


def unpack(packed, count, per=16):
    heads, rows, _ = packed.shape

    def kernel(x, *outs):
        for a in range(count):
            for j in range(per):
                outs[a][:, j * B : (j + 1) * B] = x[j, a * B : (a + 1) * B, :]

    return pl.pallas_call(
        kernel,
        grid=(heads // per,),
        in_specs=[pl.BlockSpec((per, rows, B), lambda i: (i, 0, 0))],
        out_specs=[pl.BlockSpec((B, per * B), lambda i: (0, i)) for _ in range(count)],
        out_shape=[jax.ShapeDtypeStruct((B, heads * B), BF16) for _ in range(count)],
        compiler_params=params(12),
        cost_estimate=cost(0, 2 * heads * count * B * B * 2),
        name="unpack",
    )(packed)


def decay_tables(rate, tables):
    position = iota(0).astype(F32)
    tables[0] = jnp.exp(-position * rate)
    tables[1] = jnp.exp((position + 1.0) * rate)
    tables[2] = jnp.exp(-(B - 1.0 - position) * rate)


def chunk_terms(x, surges, tables, gain, n, exact=True):
    acceptance = x[n, 0:B, :].astype(F32)
    lookup = x[n, B : 2 * B, :].astype(F32)
    payload = x[n, 2 * B : 3 * B, :]
    upto = surges[0:1] + surges[1:2] + surges[2:3]
    below = surges[3:4] + surges[4:5] + surges[5:6]
    diagonal = iota(0) == iota(1)
    below_col = jnp.sum(jnp.where(diagonal, below, 0.0), axis=1, keepdims=True)
    upto_col = jnp.sum(jnp.where(diagonal, upto, 0.0), axis=1, keepdims=True)
    total = upto[:, B - 1 : B]
    lower = iota(1) < iota(0)
    fade = jnp.where(lower, jnp.exp(below_col - upto), 0.0)
    entered = jnp.exp(below_col)
    leaving = jnp.exp(total - upto_col)
    queries = acceptance * tables[0]
    keys = lookup * tables[1]
    keys_end = lookup * tables[2] * leaving
    bonus = jnp.sum(acceptance * gain * lookup, axis=1, keepdims=True)
    if exact:
        queries_s, keys_s = split(queries), split(keys)
        keys_end_s = split(keys_end)
        scores = dot3(queries_s, keys_s, NT)
    else:
        queries_s, keys_s = queries.astype(BF16), keys.astype(BF16)
        keys_end_s = keys_end.astype(BF16)
        scores = dot(queries_s, keys_s, NT)
    scores = scores * fade + jnp.where(diagonal, bonus, 0.0)
    return dict(
        acceptance=acceptance,
        lookup=lookup,
        payload=payload,
        fade=fade,
        entered=entered,
        leaving=leaving,
        total=jnp.exp(total),
        queries=queries,
        queries_s=queries_s,
        keys_s=keys_s,
        keys_end=keys_end,
        keys_end_s=keys_end_s,
        scores=scores,
    )


def head_rows(index, fading, gain):
    return jnp.exp(fading[pl.ds(index, 1), :]), gain[pl.ds(index, 1), :]


def attention_weights(keys, queries, step, weights, n):
    scores_all = dot(keys, queries, NT)
    early = iota(0) > iota(1)
    causal = iota(0) <= iota(1)
    for sub in range(2):
        lanes = slice(sub * B, (sub + 1) * B)
        scores = []
        for j in range(REACH + 1):
            score = scores_all[(sub + j) * B : (sub + j + 1) * B, lanes]
            if j == REACH:
                keep = causal
            else:
                keep = 2 * step + sub + j >= REACH
                if j == 0:
                    keep = early & keep
            scores.append(jnp.where(keep, score, NEG))
        highest = jnp.max(functools.reduce(jnp.maximum, scores), axis=0, keepdims=True)
        raised = [jnp.exp2((score - highest) * (INV_ROOT * LOG2E)) for score in scores]
        share = 1.0 / jnp.sum(sum(raised), axis=0, keepdims=True)
        for j in range(REACH + 1):
            weights[n, (sub + j) * B : (sub + j + 1) * B, lanes] = (raised[j] * share).astype(BF16)
    weights[n, PAD + B :, 0:B] = jnp.zeros((B, B), BF16)
    weights[n, 0:B, B:] = jnp.zeros((B, B), BF16)


def forward(received, index, fading, gain, per=8):
    blocks, rows, _ = received.shape

    def kernel(
        index_ref, x, fading_ref, gain_ref, mixed, module, states, weights, turned,
        tables, memory, kring,
    ):
        rate, gain_row = head_rows(index_ref[0], fading_ref, gain_ref)
        grid_step = pl.program_id(0)

        @pl.when(grid_step == 0)
        def _():
            decay_tables(rate, tables)
            memory[...] = jnp.zeros_like(memory)
            kring[0:PAD, :] = jnp.zeros((PAD, B), BF16)

        whole = jnp.exp(-float(B) * rate)
        state = memory[...]
        for n in range(per):
            keys = x[n, KEYS : KEYS + B, :]
            kring[pl.ds(pl.multiple_of(PAD + (grid_step * per + n) * B, B), B), :] = keys
            turned[n] = keys.T
            c = chunk_terms(
                x, x[n, SPIKES : SPIKES + SPIKE_ROWS, :].astype(F32), tables, gain_row, n
            )
            states[n] = state
            out = dot_a(split(c["scores"]), c["payload"], NN) + c["entered"] * dot3(
                c["queries_s"], split(state), NT
            )
            state = state * (whole * c["total"]) + dot_b(c["payload"], c["keys_end_s"], TN)
            module[n] = out
            average = jnp.mean(out, axis=1, keepdims=True)
            centered = out - average
            variance = jnp.mean(centered * centered, axis=1, keepdims=True)
            mixed[n] = (centered * lax.rsqrt(variance + EPSILON)).astype(BF16)
            if n % 2:
                step = grid_step * (per // 2) + n // 2
                attention_weights(
                    kring[pl.ds(pl.multiple_of(step * TWO, TWO), SPAN), :],
                    jnp.concatenate(
                        [x[n - 1, QUERIES : QUERIES + B, :], x[n, QUERIES : QUERIES + B, :]], axis=0
                    ),
                    step,
                    weights,
                    n // 2,
                )
        memory[...] = state

    block = lambda: pl.BlockSpec((per, B, B), lambda i: (i, 0, 0))
    whole_array = lambda a: pl.BlockSpec(a.shape, lambda i: (0, 0))
    return pl.pallas_call(
        kernel,
        grid=(blocks // per,),
        in_specs=[
            smem(),
            pl.BlockSpec((per, rows, B), lambda i: (i, 0, 0)),
            whole_array(fading),
            whole_array(gain),
        ],
        out_specs=[
            block(),
            block(),
            block(),
            pl.BlockSpec((per // 2, SPAN, TWO), lambda i: (i, 0, 0)),
            block(),
        ],
        out_shape=[
            jax.ShapeDtypeStruct((blocks, B, B), BF16),
            jax.ShapeDtypeStruct((blocks, B, B), F32),
            jax.ShapeDtypeStruct((blocks, B, B), F32),
            jax.ShapeDtypeStruct((blocks // 2, SPAN, TWO), BF16),
            jax.ShapeDtypeStruct((blocks, B, B), BF16),
        ],
        scratch_shapes=[
            pltpu.VMEM((3, B, B), F32),
            pltpu.VMEM((B, B), F32),
            pltpu.VMEM((PAD + blocks * B, B), BF16),
        ],
        compiler_params=params(),
        cost_estimate=cost(2e10, 18 << 20),
        name="forward",
    )(index, received, fading, gain)


def pair_of(ref, at):
    return jnp.concatenate([ref[2 * at], ref[2 * at + 1]], axis=0)


def mix_backward(received, weights, cots, module, states, index, fading, gain, per=4):
    blocks = received.shape[0]
    rows = SUMS + SPIKE_ROWS
    steps = blocks // per

    def kernel(
        index_ref, x, surge_ref, w0_ref, w1_ref, w2_ref, cot_ref, module_ref, states_ref, fading_ref, gain_ref,
        out, tables, memory, sums,
    ):
        rate, gain_row = head_rows(index_ref[0], fading_ref, gain_ref)

        @pl.when(pl.program_id(0) == 0)
        def _():
            decay_tables(rate, tables)
            memory[...] = jnp.zeros_like(memory)
            sums[...] = jnp.zeros_like(sums)

        whole = jnp.exp(-float(B) * rate)
        position = iota(0).astype(F32)
        distance = jnp.maximum(iota(0) - iota(1) - 1, 0).astype(F32)
        d_state = memory[...]
        d_rate = jnp.zeros((1, B), F32)
        d_gain = jnp.zeros((1, B), F32)
        first = (steps - 1 - pl.program_id(0)) * per
        for n in reversed(range(per)):
            if n % 2:
                pair_at = first // 2 + n // 2
                g_pair = pair_of(cot_ref, pair_at).astype(F32)
                for later in range(3):
                    at = jnp.minimum(pair_at + later, blocks // 2 - 1)
                    seen = pair_of(cot_ref, at)
                    if later:
                        seen = jnp.where(pair_at + later < blocks // 2, seen, jnp.zeros_like(seen))
                    seen_by = (w2_ref, w1_ref, w0_ref)[later]
                    g_pair = g_pair + dot(seen_by[at], seen, NN)
            g = g_pair[B:] if n % 2 else g_pair[0:B]
            c = chunk_terms(x, surge_ref[n].astype(F32), tables, gain_row, n, False)
            value = module_ref[n]
            centered = value - jnp.mean(value, axis=1, keepdims=True)
            variance = jnp.mean(centered * centered, axis=1, keepdims=True)
            scale = lax.rsqrt(variance + EPSILON)
            normed = centered * scale
            grad = scale * (
                g
                - jnp.mean(g, axis=1, keepdims=True)
                - normed * jnp.mean(g * normed, axis=1, keepdims=True)
            )
            grad_s = grad.astype(BF16)
            state = states_ref[n]
            d_state_s = d_state.astype(BF16)
            payload = c["payload"]
            paired = dot(grad_s, payload, NT) * c["fade"]
            paired_s = paired.astype(BF16)
            own = jnp.sum(grad * payload.astype(F32), axis=1, keepdims=True)
            inter = c["entered"] * dot(grad_s, state.astype(BF16), NN)
            d_queries = dot(paired_s, c["keys_s"], NN) + inter
            d_keys = dot(paired_s, c["queries_s"], TN)
            d_end = dot(payload, d_state_s, NN)
            d_payload = dot(c["scores"].astype(BF16), grad_s, TN) + dot(
                c["keys_end_s"], d_state_s, NT
            )
            out[first + n, 0:B, :] = (
                d_queries * tables[0] + own * gain_row * c["lookup"]
            ).astype(BF16)
            out[first + n, B : 2 * B, :] = (
                d_keys * tables[1]
                + d_end * (tables[2] * c["leaving"])
                + own * gain_row * c["acceptance"]
            ).astype(BF16)
            out[first + n, 2 * B : 3 * B, :] = d_payload.astype(BF16)
            d_gain += jnp.sum(own * c["acceptance"] * c["lookup"], axis=0, keepdims=True)
            spread = dot((paired * distance).astype(BF16), c["keys_s"], NN)
            carried = whole * c["total"]
            d_rate += jnp.sum(
                c["queries"] * (spread + position * inter)
                + (B - 1.0 - position) * c["keys_end"] * d_end
                + (float(B) * carried) * state * d_state,
                axis=0,
                keepdims=True,
            )
            d_state = d_state * carried + dot(
                (grad * c["entered"]).astype(BF16), c["queries_s"], TN
            )
        memory[...] = d_state
        sums[0:1, :] += -rate * d_rate
        sums[1:2, :] += d_gain

        @pl.when(pl.program_id(0) == steps - 1)
        def _():
            tile = three_parts([sums[0:1, :], sums[1:2, :]])
            for b in range(blocks):
                out[b, SUMS:, :] = tile

    back = lambda i: (steps - 1 - i, 0, 0)
    block = lambda: pl.BlockSpec((per, B, B), back)
    whole_array = lambda a: pl.BlockSpec(a.shape, lambda i: (0, 0))
    return pl.pallas_call(
        kernel,
        grid=(steps,),
        in_specs=[
            smem(),
            pl.BlockSpec((per, SUMS, B), back),
            pl.BlockSpec((per, SPIKE_ROWS, B), lambda i: (steps - 1 - i, SPIKES // SPIKE_ROWS, 0)),
            *(
                pl.BlockSpec((blocks // 2, TWO, TWO), functools.partial(lambda j, i: (0, j, 0), j))
                for j in range(3)
            ),
            pl.BlockSpec(cots.shape, lambda i: (0, 0, 0)),
            block(),
            block(),
            whole_array(fading),
            whole_array(gain),
        ],
        out_specs=vmem(),
        out_shape=jax.ShapeDtypeStruct((blocks, rows, B), BF16),
        scratch_shapes=[
            pltpu.VMEM((3, B, B), F32),
            pltpu.VMEM((B, B), F32),
            pltpu.VMEM((8, B), F32),
        ],
        compiler_params=params(),
        cost_estimate=cost(2e10, 12 << 20),
        name="mix_backward",
    )(index, received, received, weights, weights, weights, cots, module, states, fading, gain)


def attention_grads(received, turned, weights, mixed, cots, per=4):
    blocks = received.shape[0]
    steps = blocks // 2 // per
    group = 2 * per

    def kernel(x, turned_ref, w0_ref, w1_ref, w2_ref, m_ref, cot_ref, out, dk, buf, sem):
        grid_step = pl.program_id(0)

        def leaving(b):
            return pltpu.make_async_copy(buf.at[b], out.at[b], sem.at[b])

        @pl.when(grid_step == 0)
        def _():
            dk[...] = jnp.zeros_like(dk)

        for n in range(per):
            step = grid_step * per + n
            window = [jnp.maximum(2 * step - REACH + j, 0) for j in range(REACH + 2)]
            queries = jnp.concatenate([x[2 * n], x[2 * n + 1]], axis=0)
            cot = jnp.concatenate([cot_ref[2 * n], cot_ref[2 * n + 1]], axis=0)
            dp = dot(jnp.concatenate([m_ref[b] for b in window], axis=0), cot, NT)
            w_all = jnp.concatenate([w0_ref[n], w1_ref[n], w2_ref[n]], axis=0)
            columns = []
            for sub in range(2):
                lanes = slice(sub * B, (sub + 1) * B)
                rows = slice(sub * B, sub * B + PAD + B)
                w = w_all[rows, lanes].astype(F32)
                g = dp[rows, lanes]
                ds = (w * (g - jnp.sum(w * g, axis=0, keepdims=True))).astype(BF16)
                zero = jnp.zeros((B, B), BF16)
                columns.append(jnp.concatenate([zero, ds] if sub else [ds, zero], axis=0))
            ds = jnp.concatenate(columns, axis=1)
            dk[pl.ds(pl.multiple_of(step * TWO, TWO), SPAN), :] += dot(ds, queries, NN)
            keys_t = jnp.concatenate([turned_ref[b] for b in window], axis=1)
            dq = (dot(keys_t, ds, NN) * INV_ROOT).T.astype(BF16)
            buf[2 * step, 0:B, :] = dq[0:B]
            buf[2 * step + 1, 0:B, :] = dq[B:]

        def finish(b):
            at = pl.ds(pl.multiple_of(PAD + b * B, B), B)
            buf[b, B:TWO, :] = (dk[at, :] * INV_ROOT).astype(BF16)
            leaving(b).start()

        for j in range(group):
            b = grid_step * group - REACH + j

            @pl.when(b >= 0)
            def _(b=b):
                finish(b)

        @pl.when(grid_step == steps - 1)
        def _():
            for b in range(blocks - REACH, blocks):
                finish(b)
            for b in range(blocks):
                leaving(b).wait()

    everything = lambda a: pl.BlockSpec(a.shape, lambda i: (0, 0, 0))
    return pl.pallas_call(
        kernel,
        grid=(steps,),
        in_specs=[
            pl.BlockSpec((group, B, B), lambda i: (i, QUERIES // B, 0)),
            everything(turned),
            *(
                pl.BlockSpec((per, TWO, TWO), functools.partial(lambda j, i: (i, j, 0), j))
                for j in range(3)
            ),
            everything(mixed),
            pl.BlockSpec((group, B, B), lambda i: (i, 0, 0)),
        ],
        out_specs=pl.BlockSpec(memory_space=pl.ANY),
        out_shape=jax.ShapeDtypeStruct((blocks, TWO, B), BF16),
        scratch_shapes=[
            pltpu.VMEM((PAD + blocks * B, B), F32),
            pltpu.VMEM((blocks, TWO, B), BF16),
            pltpu.SemaphoreType.DMA((blocks,)),
        ],
        compiler_params=params(),
        cost_estimate=cost(2e10, 14 << 20),
        name="attention_grads",
    )(received, turned, weights, weights, weights, mixed, cots)


def exchange(blocks):
    return lax.all_to_all(blocks, "seq", 0, 0, tiled=True)


def local(
    probe_matrix,
    softmax_lookup_matrix,
    acceptance_gate,
    recurrent_lookup_matrix,
    recurrent_payload_matrix,
    upstream_adjoint,
    feature_fading_exponent,
    diagonal_reward_factor,
    spike_fading_exponent,
):
    positions = probe_matrix.shape[1] * lax.axis_size("seq") * lax.axis_size("dp")
    here = lax.axis_index("seq")
    index = here.astype(jnp.int32).reshape(1)
    first_out, cots_out = pack(
        (
            acceptance_gate[0],
            recurrent_lookup_matrix[0],
            recurrent_payload_matrix[0],
            probe_matrix[0],
            softmax_lookup_matrix[0],
        ),
        upstream_adjoint[0],
        spike_fading_exponent[0].T,
    )
    first_out, cots_out, index = lax.optimization_barrier((first_out, cots_out, index))
    first_in = exchange(first_out)
    first_in, cots_out = lax.optimization_barrier((first_in, cots_out))
    cots = exchange(cots_out)
    mixed, module, states, weights, turned = forward(
        first_in, index, feature_fading_exponent, diagonal_reward_factor
    )
    att_back = exchange(attention_grads(first_in, turned, weights, mixed, cots))
    mix_out = mix_backward(
        first_in, weights, cots, module, states, index, feature_fading_exponent, diagonal_reward_factor
    )
    mix_out, att_back = lax.optimization_barrier((mix_out, att_back))
    mix_back = exchange(mix_out)
    dq, dk = unpack(att_back, 2)
    mix_back, dq, dk = lax.optimization_barrier((mix_back, dq, dk))
    parts = mix_back[:, SUMS : SUMS + 6, :].astype(F32)
    sums = jnp.stack(
        [parts[:, 0] + parts[:, 1] + parts[:, 2], parts[:, 3] + parts[:, 4] + parts[:, 5]]
    )
    group = lax.axis_size("dp")
    for bit in range(group.bit_length() - 1):
        sums = sums + lax.ppermute(sums, "dp", [(i, i ^ (1 << bit)) for i in range(group)])
    adjoints = sums * positions ** (-0.5)
    dr, dmk, dmv = unpack(mix_back, 3)
    return (dq[None], dk[None], dr[None], dmk[None], dmv[None], adjoints[0], adjoints[1])


def solution(mesh):
    rows = P("dp", "seq", None)
    return jax.shard_map(
        local,
        mesh=mesh,
        in_specs=(rows,) * 6 + (P(), P(), rows),
        out_specs=(rows,) * 5 + (P(), P()),
        check_vma=False,
    )
```

time: 224 us -> 210 us (0.938)
  blocking collectives: 46.2 us -> 72.4 us
  waiting for transfers between devices: 67.8 us -> 41.7 us
  Pallas kernels: 69.8 us -> 61.8 us
  starting transfers between devices: 31.8 us -> 28.2 us
    all_to_all x3, waiting for transfers between devices: 67.8 us -> 40.8 us  [exchange(): return lax.all_to_all(blocks, 'seq', 0, 0, tiled=True)]
    all_to_all x1, blocking collectives: 46.2 us -> 72.4 us  [exchange(): return lax.all_to_all(blocks, 'seq', 0, 0, tiled=True)]
    pallas_call x1, Pallas kernels: 25.1 us -> 21.4 us  [mix_backward(): pl.pallas_call(kernel, grid=(steps,), in_specs=[smem(), pl.BlockSpec((per...]
    all_to_all x3, starting transfers between devices: 23.9 us -> 20.3 us  [exchange(): return lax.all_to_all(blocks, 'seq', 0, 0, tiled=True)]
    pallas_call x2, Pallas kernels: 6.31 us -> 3.65 us  [unpack(): pl.pallas_call(kernel, grid=(heads // per,), in_specs=[pl.BlockSpec((per,...]
    pallas_call x4 -> x3, Pallas kernels: 38.4 us -> 36.8 us  [the longest x1 17.6 us: forward(): pl.pallas_call(kernel, grid=(blocks // per,), in_specs=[smem(), pl.BlockS...]
    ppermute x3 -> x2, starting transfers between devices: 7.82 us -> 7.9 us  [local(): lax.ppermute(sums, 'dp', [(i, i ^ 1 << bit) for i in range(group)])]
  transfers between devices with their start and end apart: 6 -> 5, of which waited for: 2 -> 3; matrix products, arithmetic and copies ran while one was open for 0% -> 0% of each run, Pallas kernels for 20% -> 20%
where the time goes in v2:
time: 210 us; the launch traced here: 209 us
  blocking collectives  72.4 us (34%)
  Pallas kernels  61.8 us (29%)
  waiting for transfers between devices  41.7 us (20%)
  starting transfers between devices  28.2 us (13%)
  local copies, waits for them, and re-layouts  4.49 us (2%)
    all_to_all x1, blocking collectives, exchange(): return lax.all_to_all(blocks, 'seq', 0, 0, tiled=True)  72.4 us
    all_to_all x3, waiting for transfers between devices, exchange(): return lax.all_to_all(blocks, 'seq', 0, 0, tiled=True)  40.8 us
    pallas_call x1, Pallas kernels, mix_backward(): pl.pallas_call(kernel, grid=(steps,), in_specs=[smem(), pl.BlockSpec((per...  21.4 us
    all_to_all x3, starting transfers between devices, exchange(): return lax.all_to_all(blocks, 'seq', 0, 0, tiled=True)  20.3 us
    pallas_call x1, Pallas kernels, forward(): pl.pallas_call(kernel, grid=(blocks // per,), in_specs=[smem(), pl.BlockS...  17.6 us
    pallas_call x1, Pallas kernels, attention_grads(): pl.pallas_call(kernel, grid=(steps,), in_specs=[pl.BlockSpec((group, B, B...  12.9 us
    ppermute x2, starting transfers between devices, local(): lax.ppermute(sums, 'dp', [(i, i ^ 1 << bit) for i in range(group)])  7.9 us
    pallas_call x1, Pallas kernels, pack(): pl.pallas_call(kernel, grid=(steps,), in_specs=[pl.BlockSpec((B, per * B)...  6.24 us
  transfers between devices with their start and end apart: 5, of which 3 were waited for; matrix products, arithmetic and copies ran while one was open for 0% of the time, Pallas kernels for 20%

profile of v2, /device:TPU:1, one launch (start us, length us, event | category | flops | bytes accessed | tf_op | source)
XLA Modules:
  0.0 209.4 jit_solution(11498898953592304162)
XLA Ops:
  0.6 6.2 %pack.1 = (bf16[32,656,128]{2,1,0:T(8,128)(2,1)}, bf16[32,128,128]{2,1,0:T(8,128)(2,1)}) custom-call(bf16[128,4096]{1,0:T(8,128)(2,1)} %bitcast.25, bf16[128,4096]{1,0:T(8,128)(2,1)} %bitcast.26, bf16[128,4096]{1,0:T(8,128)(2,1)} %bitcast.27, bf16[128,4096]{1,0:T(8,128)(2,1)} %bitcast.28, bf16[128,4096]{1,0:T(8,128)(2,1)} %bitcast.29, ...), custom_call_target="tpu_custom_call" | custom-call | bytes 12845056 | tf_op jit(solution)/shard_map/pack/pallas_call | solution.py:129
  6.9 72.4 %all_to_all.20.x.surge_ref = bf16[32,656,128]{2,1,0:T(8,128)(2,1)} all-to-all(bf16[32,656,128]{2,1,0:T(8,128)(2,1)} %get-tuple-element.32), channel_id=1, replica_groups=mesh['seq'=32,'dp'=4] {'seq'}, dimensions={0} | all-to-all | bytes 10747904 | tf_op jit(solution)/shard_map/all_to_all | solution.py:551
  79.3 4.0 %all-to-all-start.1 = ((bf16[32,128,128]{2,1,0:T(8,128)(2,1)}), bf16[32,128,128]{2,1,0:T(8,128)(2,1)S(1)}, u32[]{:S(2)}, u32[]{:S(2)}) async-start(bf16[32,128,128]{2,1,0:T(8,128)(2,1)} %get-tuple-element.36), calls=%async_computation.1 | async-start | bytes 2097152 | tf_op jit(solution)/shard_map/all_to_all | solution.py:551
  83.2 17.6 %forward.1 = (bf16[32,128,128]{2,1,0:T(8,128)(2,1)}, f32[32,128,128]{2,1,0:T(8,128)}, f32[32,128,128]{2,1,0:T(8,128)}, bf16[16,768,256]{2,1,0:T(8,128)(2,1)}, bf16[32,128,128]{2,1,0:T(8,128)(2,1)}) custom-call(s32[1]{0:T(128)} %bitcast.8.index_ref, bf16[32,656,128]{2,1,0:T(8,128)(2,1)} %all_to_all.20.x.surge_ref, f32[32,128]{1,0:T(8,128)} %fading_ref.3, ...), custom_call_target="tpu_custom_call" | custom-call | flops 20000000000 | bytes 18874368 | tf_op jit(solution)/shard_map/forward/pallas_call | solution.py:302
  100.8 0.0 all-to-all-done.1.cot_ref
  100.8 0.0 copy-start.2
  100.8 1.0 copy-done.2
  101.8 12.9 %attention_grads.1 = bf16[32,256,128]{2,1,0:T(8,128)(2,1)} custom-call(bf16[32,656,128]{2,1,0:T(8,128)(2,1)} %all_to_all.20.x.surge_ref, bf16[32,128,128]{2,1,0:T(8,128)(2,1)} %get-tuple-element.39.turned_ref, bf16[16,768,256]{2,1,0:T(8,128)(2,1)} %get-tuple-element.35.w0_ref.w1_ref.w2_ref, bf16[16,768,256]{2,1,0:T(8,128)(2,1)} %get-tuple-element.35.w0_ref.w1_ref.w2_ref, ...), custom_call_target="tpu_custom_call" | custom-call | flops 20000000000 | bytes 14680064 | tf_op jit(solution)/shard_map/attention_grads/pallas_call | solution.py:524
  114.8 7.7 %all-to-all-start.2 = ((bf16[32,256,128]{2,1,0:T(8,128)(2,1)}), bf16[32,256,128]{2,1,0:T(8,128)(2,1)S(1)}, u32[]{:S(2)}, u32[]{:S(2)}) async-start(bf16[32,256,128]{2,1,0:T(8,128)(2,1)} %attention_grads.1), calls=%async_computation.2 | async-start | bytes 4194304 | tf_op jit(solution)/shard_map/all_to_all | solution.py:551
  122.5 21.4 %mix_backward.1 = bf16[32,400,128]{2,1,0:T(8,128)(2,1)} custom-call(s32[1]{0:T(128)} %bitcast.8.index_ref, bf16[32,656,128]{2,1,0:T(8,128)(2,1)} %all_to_all.20.x.surge_ref, bf16[32,656,128]{2,1,0:T(8,128)(2,1)} %all_to_all.20.x.surge_ref, bf16[16,768,256]{2,1,0:T(8,128)(2,1)} %get-tuple-element.35.w0_ref.w1_ref.w2_ref, ...), custom_call_target="tpu_custom_call" | custom-call | flops 20000000000 | bytes 12582912 | tf_op jit(solution)/shard_map/mix_backward/pallas_call | solution.py:436
  143.9 2.4 %all-to-all-done.2.x = bf16[32,256,128]{2,1,0:T(8,128)(2,1)S(1)} async-done(((bf16[32,256,128]{2,1,0:T(8,128)(2,1)}), bf16[32,256,128]{2,1,0:T(8,128)(2,1)S(1)}, u32[]{:S(2)}, u32[]{:S(2)}) %all-to-all-start.2) | async-done | bytes 2097184 | tf_op jit(solution)/shard_map/all_to_all | solution.py:551
  146.3 1.3 copy-done
  147.7 8.6 %all-to-all-start.3 = ((bf16[32,400,128]{2,1,0:T(8,128)(2,1)}), bf16[32,400,128]{2,1,0:T(8,128)(2,1)S(1)}, u32[]{:S(2)}, u32[]{:S(2)}) async-start(bf16[32,400,128]{2,1,0:T(8,128)(2,1)} %mix_backward.1), calls=%async_computation.3 | async-start | bytes 6553600 | tf_op jit(solution)/shard_map/all_to_all | solution.py:551
  156.3 0.0 copy-start.1
  156.3 1.6 copy-done.1
  157.9 1.6 unpack.2
  159.5 38.4 %all-to-all-done.3.x = bf16[32,400,128]{2,1,0:T(8,128)(2,1)S(1)} async-done(((bf16[32,400,128]{2,1,0:T(8,128)(2,1)}), bf16[32,400,128]{2,1,0:T(8,128)(2,1)S(1)}, u32[]{:S(2)}, u32[]{:S(2)}) %all-to-all-start.3) | async-done | bytes 3276832 | tf_op jit(solution)/shard_map/all_to_all | solution.py:551
  197.9 0.1 fusion.1
  198.0 4.6 %collective-permute-start = (f32[2,32,128]{2,1,0:T(8,128)S(1)}, f32[2,32,128]{2,1,0:T(8,128)S(1)}, u32[]{:S(2)}, u32[]{:S(2)}) collective-permute-start(f32[2,32,128]{2,1,0:T(8,128)S(1)} %pad_maximum_fusion), channel_id=1, source_target_pairs={{0,1},{1,0},{2,3},{3,2},{4,5},{5,4},{6,7},{7,6},{8,9},{9,8},{10,11... | collective-permute-start | bytes 98312 | tf_op jit(solution)/shard_map/ppermute | solution.py:600
  202.5 0.9 collective-permute-done
  203.4 3.3 %collective-permute-start.1 = (f32[2,32,128]{2,1,0:T(8,128)S(1)}, f32[2,32,128]{2,1,0:T(8,128)S(1)}, u32[]{:S(2)}, u32[]{:S(2)}) collective-permute-start(f32[2,32,128]{2,1,0:T(8,128)S(1)} %fusion), channel_id=1, source_target_pairs={{0,2},{1,3},{2,0},{3,1},{4,6},{5,7},{6,4},{7,5},{8,10},{9,11},{10,... | collective-permute-start | bytes 98312 | tf_op jit(solution)/shard_map/ppermute | solution.py:600
  206.7 2.1 unpack.3
  208.8 0.0 collective-permute-done.1
  208.8 0.6 slice_bitcast_fusion
  (6 shorter events, 0.0 us)
Async XLA Ops:
  79.3 21.6 %all-to-all-start.1 = ((bf16[32,128,128]{2,1,0:T(8,128)(2,1)}), bf16[32,128,128]{2,1,0:T(8,128)(2,1)S(1)}, u32[]{:S(2)}, u32[]{:S(2)}) async-start(bf16[32,128,128]{2,1,0:T(8,128)(2,1)} %get-tuple-element.36), calls=%async_computation.1 | async-start | bytes 2097152 | tf_op jit(solution)/shard_map/all_to_all | solution.py:551
  100.8 1.0 copy-start.2
  114.8 31.6 %all-to-all-start.2 = ((bf16[32,256,128]{2,1,0:T(8,128)(2,1)}), bf16[32,256,128]{2,1,0:T(8,128)(2,1)S(1)}, u32[]{:S(2)}, u32[]{:S(2)}) async-start(bf16[32,256,128]{2,1,0:T(8,128)(2,1)} %attention_grads.1), calls=%async_computation.2 | async-start | bytes 4194304 | tf_op jit(solution)/shard_map/all_to_all | solution.py:551
  146.3 1.3 copy-start
  147.7 50.2 %all-to-all-start.3 = ((bf16[32,400,128]{2,1,0:T(8,128)(2,1)}), bf16[32,400,128]{2,1,0:T(8,128)(2,1)S(1)}, u32[]{:S(2)}, u32[]{:S(2)}) async-start(bf16[32,400,128]{2,1,0:T(8,128)(2,1)} %mix_backward.1), calls=%async_computation.3 | async-start | bytes 6553600 | tf_op jit(solution)/shard_map/all_to_all | solution.py:551
  156.3 1.6 copy-start.1
  198.0 5.5 %collective-permute-start = (f32[2,32,128]{2,1,0:T(8,128)S(1)}, f32[2,32,128]{2,1,0:T(8,128)S(1)}, u32[]{:S(2)}, u32[]{:S(2)}) collective-permute-start(f32[2,32,128]{2,1,0:T(8,128)S(1)} %pad_maximum_fusion), channel_id=1, source_target_pairs={{0,1},{1,0},{2,3},{3,2},{4,5},{5,4},{6,7},{7,6},{8,9},{9,8},{10,11... | collective-permute-start | bytes 98312 | tf_op jit(solution)/shard_map/ppermute | solution.py:600
  203.4 5.4 %collective-permute-start.1 = (f32[2,32,128]{2,1,0:T(8,128)S(1)}, f32[2,32,128]{2,1,0:T(8,128)S(1)}, u32[]{:S(2)}, u32[]{:S(2)}) collective-permute-start(f32[2,32,128]{2,1,0:T(8,128)S(1)} %fusion), channel_id=1, source_target_pairs={{0,2},{1,3},{2,0},{3,1},{4,6},{5,7},{6,4},{7,5},{8,10},{9,11},{10,... | collective-permute-start | bytes 98312 | tf_op jit(solution)/shard_map/ppermute | solution.py:600

commit v3 on v2

--- a/solution.py
+++ b/solution.py
@@ -15,7 +15,7 @@
 LOG2E = math.log2(math.e)
 B = 128
 REACH = 4
-SPIKE_ROWS = 16
+SPIKE_ROWS = 8
 QUERIES = 3 * B
 KEYS = 4 * B
 SPIKES = 5 * B
@@ -81,67 +81,75 @@
     return tile.astype(BF16)
 
 
-def pack(arrays, cots, spike, per=8):
+def pack(arrays, cots, spike, per=4):
     heads = cots.shape[1] // B
-    count = len(arrays)
-    steps = heads // per
+    count = len(arrays) + 1
+    groups = heads // per
     rows = SPIKES + SPIKE_ROWS
 
     def kernel(*refs):
-        sources, surge_ref = refs[: count + 1], refs[count + 1]
-        first, second, first_buf, second_buf, sums, first_sem, second_sem = refs[count + 2 :]
-        step = pl.program_id(0)
-
-        def leaving(h):
-            return pltpu.make_async_copy(first_buf.at[h], first.at[h], first_sem.at[h])
+        sources, surge_ref = refs[:count], refs[count]
+        first_out, second, first, held, second_buf, sums, in_sem, out_sem = refs[count + 1 :]
+
+        def entering(a, g):
+            columns = slice(g * per * B, (g + 1) * per * B)
+            return pltpu.make_async_copy(
+                sources[a].at[:, columns], held.at[a, :, columns], in_sem.at[a * groups + g]
+            )
+
+        def leaving(g):
+            at = slice(g * per, (g + 1) * per)
+            return pltpu.make_async_copy(first.at[at], first_out.at[at], out_sem.at[g])
 
         def leaving_cots(g):
-            at = pl.ds(g * per, per)
-            return pltpu.make_async_copy(second_buf.at[at], second.at[at], second_sem.at[g])
-
-        @pl.when(step == 0)
-        def _():
-            surge = surge_ref[...]
-            upto = jnp.where(iota(0) <= iota(1), 1.0, 0.0).astype(F32)
-            below = jnp.where(iota(0) < iota(1), 1.0, 0.0).astype(F32)
-            for n, mask in enumerate((upto, below)):
-                sums[n] = lax.dot_general(
-                    surge, mask, NN, precision=lax.Precision.HIGHEST, preferred_element_type=F32
-                )
-
-        for j in range(per):
-            h = step * per + j
-            columns = slice(j * B, (j + 1) * B)
-            for a in range(count):
-                first_buf[h, a * B : (a + 1) * B, :] = sources[a][:, columns]
-            first_buf[h, SPIKES:, :] = three_parts([sums[n, pl.ds(h, 1), :] for n in range(2)])
-            leaving(h).start()
-            second_buf[h] = sources[count][:, columns]
-        leaving_cots(step).start()
-
-        @pl.when(step == steps - 1)
-        def _():
-            for h in range(heads):
-                leaving(h).wait()
-            for g in range(steps):
-                leaving_cots(g).wait()
-
+            at = slice(g * per, (g + 1) * per)
+            return pltpu.make_async_copy(second_buf.at[at], second.at[at], out_sem.at[groups + g])
+
+        for g in range(groups):
+            for a in range(count - 1):
+                entering(a, g).start()
+        for g in range(groups):
+            entering(count - 1, g).start()
+        surge = surge_ref[...]
+        upto = jnp.where(iota(0) <= iota(1), 1.0, 0.0).astype(F32)
+        below = jnp.where(iota(0) < iota(1), 1.0, 0.0).astype(F32)
+        for n, mask in enumerate((upto, below)):
+            sums[n] = lax.dot_general(
+                surge, mask, NN, precision=lax.Precision.HIGHEST, preferred_element_type=F32
+            )
+        for h in range(heads):
+            first[h, SPIKES:, :] = three_parts([sums[n, h : h + 1, :] for n in range(2)])
+        for g in range(groups):
+            for a in range(count - 1):
+                entering(a, g).wait()
+                for h in range(g * per, (g + 1) * per):
+                    first[h, a * B : (a + 1) * B, :] = held[a, :, h * B : (h + 1) * B]
+            leaving(g).start()
+        for g in range(groups):
+            entering(count - 1, g).wait()
+            for h in range(g * per, (g + 1) * per):
+                second_buf[h] = held[count - 1, :, h * B : (h + 1) * B]
+            leaving_cots(g).start()
+        for g in range(groups):
+            leaving(g).wait()
+            leaving_cots(g).wait()
+
+    hbm = pl.BlockSpec(memory_space=pl.ANY)
     return pl.pallas_call(
         kernel,
-        grid=(steps,),
-        in_specs=[pl.BlockSpec((B, per * B), lambda i: (0, i)) for _ in range(count + 1)]
-        + [pl.BlockSpec(spike.shape, lambda i: (0, 0))],
-        out_specs=[pl.BlockSpec(memory_space=pl.ANY)] * 2,
+        in_specs=[hbm] * count + [vmem()],
+        out_specs=[hbm, hbm],
         out_shape=[
             jax.ShapeDtypeStruct((heads, rows, B), BF16),
             jax.ShapeDtypeStruct((heads, B, B), BF16),
         ],
         scratch_shapes=[
             pltpu.VMEM((heads, rows, B), BF16),
+            pltpu.VMEM((count, B, heads * B), BF16),
             pltpu.VMEM((heads, B, B), BF16),
             pltpu.VMEM((2, heads, B), F32),
-            pltpu.SemaphoreType.DMA((heads,)),
-            pltpu.SemaphoreType.DMA((steps,)),
+            pltpu.SemaphoreType.DMA((count * groups,)),
+            pltpu.SemaphoreType.DMA((2 * groups,)),
         ],
         compiler_params=params(),
         cost_estimate=cost(0, 2 * heads * (rows + B) * B * 2),
@@ -149,24 +157,28 @@
     )(*arrays, cots, spike)
 
 
-def unpack(packed, count, per=16):
-    heads, rows, _ = packed.shape
-
-    def kernel(x, *outs):
-        for a in range(count):
-            for j in range(per):
-                outs[a][:, j * B : (j + 1) * B] = x[j, a * B : (a + 1) * B, :]
+def unpack(packs, counts, per=16):
+    heads = packs[0].shape[0]
+    total = sum(counts)
+
+    def kernel(*refs):
+        outs = iter(refs[len(packs) :])
+        for x, count in zip(refs, counts):
+            for a in range(count):
+                out = next(outs)
+                for j in range(per):
+                    out[:, j * B : (j + 1) * B] = x[j, a * B : (a + 1) * B, :]
 
     return pl.pallas_call(
         kernel,
         grid=(heads // per,),
-        in_specs=[pl.BlockSpec((per, rows, B), lambda i: (i, 0, 0))],
-        out_specs=[pl.BlockSpec((B, per * B), lambda i: (0, i)) for _ in range(count)],
-        out_shape=[jax.ShapeDtypeStruct((B, heads * B), BF16) for _ in range(count)],
-        compiler_params=params(12),
-        cost_estimate=cost(0, 2 * heads * count * B * B * 2),
+        in_specs=[pl.BlockSpec((per, x.shape[1], B), lambda i: (i, 0, 0)) for x in packs],
+        out_specs=[pl.BlockSpec((B, per * B), lambda i: (0, i)) for _ in range(total)],
+        out_shape=[jax.ShapeDtypeStruct((B, heads * B), BF16) for _ in range(total)],
+        compiler_params=params(20),
+        cost_estimate=cost(0, 2 * heads * total * B * B * 2),
         name="unpack",
-    )(packed)
+    )(*packs)
 
 
 def decay_tables(rate, tables):
@@ -327,7 +339,7 @@
             pltpu.VMEM((B, B), F32),
             pltpu.VMEM((PAD + blocks * B, B), BF16),
         ],
-        compiler_params=params(),
+        compiler_params=params(63),
         cost_estimate=cost(2e10, 18 << 20),
         name="forward",
     )(index, received, fading, gain)
@@ -384,19 +396,20 @@
                 - jnp.mean(g, axis=1, keepdims=True)
                 - normed * jnp.mean(g * normed, axis=1, keepdims=True)
             )
-            grad_s = grad.astype(BF16)
+            grad_2 = split(grad)
+            grad_s = grad_2[0]
             state = states_ref[n]
             d_state_s = d_state.astype(BF16)
             payload = c["payload"]
-            paired = dot(grad_s, payload, NT) * c["fade"]
+            paired = dot_a(grad_2, payload, NT) * c["fade"]
             paired_s = paired.astype(BF16)
             own = jnp.sum(grad * payload.astype(F32), axis=1, keepdims=True)
             inter = c["entered"] * dot(grad_s, state.astype(BF16), NN)
             d_queries = dot(paired_s, c["keys_s"], NN) + inter
             d_keys = dot(paired_s, c["queries_s"], TN)
             d_end = dot(payload, d_state_s, NN)
-            d_payload = dot(c["scores"].astype(BF16), grad_s, TN) + dot(
-                c["keys_end_s"], d_state_s, NT
+            d_payload = dot_b(c["scores"].astype(BF16), grad_2, TN) + dot_b(
+                c["keys_end_s"], split(d_state), NT
             )
             out[first + n, 0:B, :] = (
                 d_queries * tables[0] + own * gain_row * c["lookup"]
@@ -478,12 +491,15 @@
         def _():
             dk[...] = jnp.zeros_like(dk)
 
-        for n in range(per):
-            step = grid_step * per + n
-            window = [jnp.maximum(2 * step - REACH + j, 0) for j in range(REACH + 2)]
-            queries = jnp.concatenate([x[2 * n], x[2 * n + 1]], axis=0)
-            cot = jnp.concatenate([cot_ref[2 * n], cot_ref[2 * n + 1]], axis=0)
-            dp = dot(jnp.concatenate([m_ref[b] for b in window], axis=0), cot, NT)
+        def window_of(n):
+            first = 2 * (grid_step * per + n) - REACH
+            return [jnp.maximum(first + j, 0) for j in range(REACH + 2)]
+
+        def dp_of(n):
+            seen = jnp.concatenate([m_ref[b] for b in window_of(n)], axis=0)
+            return dot(seen, pair_of(cot_ref, n), NT)
+
+        def ds_of(n, dp):
             w_all = jnp.concatenate([w0_ref[n], w1_ref[n], w2_ref[n]], axis=0)
             columns = []
             for sub in range(2):
@@ -494,12 +510,25 @@
                 ds = (w * (g - jnp.sum(w * g, axis=0, keepdims=True))).astype(BF16)
                 zero = jnp.zeros((B, B), BF16)
                 columns.append(jnp.concatenate([zero, ds] if sub else [ds, zero], axis=0))
-            ds = jnp.concatenate(columns, axis=1)
-            dk[pl.ds(pl.multiple_of(step * TWO, TWO), SPAN), :] += dot(ds, queries, NN)
-            keys_t = jnp.concatenate([turned_ref[b] for b in window], axis=1)
+            return jnp.concatenate(columns, axis=1)
+
+        def emit(n, ds):
+            step = grid_step * per + n
+            dk[pl.ds(pl.multiple_of(step * TWO, TWO), SPAN), :] += dot(ds, pair_of(x, n), NN)
+            keys_t = jnp.concatenate([turned_ref[b] for b in window_of(n)], axis=1)
             dq = (dot(keys_t, ds, NN) * INV_ROOT).T.astype(BF16)
             buf[2 * step, 0:B, :] = dq[0:B]
             buf[2 * step + 1, 0:B, :] = dq[B:]
+
+        dp_next, ds_last = dp_of(0), None
+        for n in range(per):
+            dp = dp_next
+            if n + 1 < per:
+                dp_next = dp_of(n + 1)
+            if ds_last is not None:
+                emit(n - 1, ds_last)
+            ds_last = ds_of(n, dp)
+        emit(per - 1, ds_last)
 
         def finish(b):
             at = pl.ds(pl.multiple_of(PAD + b * B, B), B)
@@ -589,8 +618,7 @@
     )
     mix_out, att_back = lax.optimization_barrier((mix_out, att_back))
     mix_back = exchange(mix_out)
-    dq, dk = unpack(att_back, 2)
-    mix_back, dq, dk = lax.optimization_barrier((mix_back, dq, dk))
+    mix_back, att_back = lax.optimization_barrier((mix_back, att_back))
     parts = mix_back[:, SUMS : SUMS + 6, :].astype(F32)
     sums = jnp.stack(
         [parts[:, 0] + parts[:, 1] + parts[:, 2], parts[:, 3] + parts[:, 4] + parts[:, 5]]
@@ -599,7 +627,7 @@
     for bit in range(group.bit_length() - 1):
         sums = sums + lax.ppermute(sums, "dp", [(i, i ^ (1 << bit)) for i in range(group)])
     adjoints = sums * positions ** (-0.5)
-    dr, dmk, dmv = unpack(mix_back, 3)
+    dq, dk, dr, dmk, dmv = unpack((att_back, mix_back), (2, 3))
     return (dq[None], dk[None], dr[None], dmk[None], dmv[None], adjoints[0], adjoints[1])
 
 

time: 210 us -> 203 us (0.967)
  blocking collectives: 72.4 us -> 119 us
  waiting for transfers between devices: 41.7 us -> 1.21 us
  starting transfers between devices: 28.2 us -> 18.9 us
  local copies, waits for them, and re-layouts: 4.49 us -> 0.61 us
    all_to_all x1 -> x2, blocking collectives: 72.4 us -> 119 us  [exchange(): return lax.all_to_all(blocks, 'seq', 0, 0, tiled=True)]
    all_to_all x3 -> x2, waiting for transfers between devices: 40.8 us -> 0.35 us  [exchange(): return lax.all_to_all(blocks, 'seq', 0, 0, tiled=True)]
    all_to_all x3 -> x2, starting transfers between devices: 20.3 us -> 12.3 us  [exchange(): return lax.all_to_all(blocks, 'seq', 0, 0, tiled=True)]
    unnamed x6 -> x0, local copies, waits for them, and re-layouts: 3.88 us -> none
    pallas_call x1, Pallas kernels: 12.9 us -> 10.4 us  [attention_grads(): pl.pallas_call(kernel, grid=(steps,), in_specs=[pl.BlockSpec((group, B, B...]
    pallas_call x1, Pallas kernels: 21.4 us -> 23.8 us  [mix_backward(): pl.pallas_call(kernel, grid=(steps,), in_specs=[smem(), pl.BlockSpec((per...]
  transfers between devices with their start and end apart: 5 -> 4, of which waited for: 3 -> 2; matrix products, arithmetic and copies ran while one was open for 0% -> 0% of each run, Pallas kernels for 20% -> 22%
where the time goes in v3:
time: 203 us; the launch traced here: 202 us
  blocking collectives  119 us (59%)
  Pallas kernels  61.3 us (30%)
  starting transfers between devices  18.9 us (9%)
    all_to_all x2, blocking collectives, exchange(): return lax.all_to_all(blocks, 'seq', 0, 0, tiled=True)  119 us
    pallas_call x1, Pallas kernels, mix_backward(): pl.pallas_call(kernel, grid=(steps,), in_specs=[smem(), pl.BlockSpec((per...  23.8 us
    pallas_call x1, Pallas kernels, forward(): pl.pallas_call(kernel, grid=(blocks // per,), in_specs=[smem(), pl.BlockS...  17.6 us
    all_to_all x2, starting transfers between devices, exchange(): return lax.all_to_all(blocks, 'seq', 0, 0, tiled=True)  12.3 us
    pallas_call x1, Pallas kernels, attention_grads(): pl.pallas_call(kernel, grid=(steps,), in_specs=[pl.BlockSpec((group, B, B...  10.4 us
    pallas_call x1, Pallas kernels, pack(): pl.pallas_call(kernel, in_specs=[hbm] * count + [vmem()], out_specs=[hbm,...  6.54 us
    ppermute x2, starting transfers between devices, local(): lax.ppermute(sums, 'dp', [(i, i ^ 1 << bit) for i in range(group)])  6.53 us
  transfers between devices with their start and end apart: 4, of which 2 were waited for; matrix products, arithmetic and copies ran while one was open for 0% of the time, Pallas kernels for 22%

profile of v3, /device:TPU:1, one launch (start us, length us, event | category | flops | bytes accessed | tf_op | source)
XLA Modules:
  0.0 202.2 jit_solution(2602467430159962397)
XLA Ops:
  0.6 6.5 %pack.1 = (bf16[32,648,128]{2,1,0:T(8,128)(2,1)}, bf16[32,128,128]{2,1,0:T(8,128)(2,1)}) custom-call(bf16[128,4096]{1,0:T(8,128)(2,1)} %bitcast.25, bf16[128,4096]{1,0:T(8,128)(2,1)} %bitcast.26, bf16[128,4096]{1,0:T(8,128)(2,1)} %bitcast.27, bf16[128,4096]{1,0:T(8,128)(2,1)} %bitcast.28, bf16[128,4096]{1,0:T(8,128)(2,1)} %bitcast.29, ...), custom_call_target="tpu_custom_call" | custom-call | bytes 12713984 | tf_op jit(solution)/shard_map/pack/pallas_call | solution.py:138
  7.2 71.9 %all_to_all.20.x.surge_ref = bf16[32,648,128]{2,1,0:T(8,128)(2,1)} all-to-all(bf16[32,648,128]{2,1,0:T(8,128)(2,1)} %get-tuple-element.31), channel_id=1, replica_groups=mesh['seq'=32,'dp'=4] {'seq'}, dimensions={0} | all-to-all | bytes 10616832 | tf_op jit(solution)/shard_map/all_to_all | solution.py:580
  79.1 4.7 %all-to-all-start.1 = ((bf16[32,128,128]{2,1,0:T(8,128)(2,1)}), bf16[32,128,128]{2,1,0:T(8,128)(2,1)}, u32[]{:S(2)}, u32[]{:S(2)}) async-start(bf16[32,128,128]{2,1,0:T(8,128)(2,1)} %get-tuple-element.35), calls=%async_computation.1 | async-start | bytes 2097152 | tf_op jit(solution)/shard_map/all_to_all | solution.py:580
  83.8 17.6 %forward.1 = (bf16[32,128,128]{2,1,0:T(8,128)(2,1)}, f32[32,128,128]{2,1,0:T(8,128)}, f32[32,128,128]{2,1,0:T(8,128)}, bf16[16,768,256]{2,1,0:T(8,128)(2,1)}, bf16[32,128,128]{2,1,0:T(8,128)(2,1)}) custom-call(s32[1]{0:T(128)} %bitcast.8.index_ref, bf16[32,648,128]{2,1,0:T(8,128)(2,1)} %all_to_all.20.x.surge_ref, f32[32,128]{1,0:T(8,128)} %fading_ref.3, ...), custom_call_target="tpu_custom_call" | custom-call | flops 20000000000 | bytes 18874368 | tf_op jit(solution)/shard_map/forward/pallas_call | solution.py:314
  101.4 0.0 all-to-all-done.1.cot_ref
  101.4 10.4 %attention_grads.1 = bf16[32,256,128]{2,1,0:T(8,128)(2,1)} custom-call(bf16[32,648,128]{2,1,0:T(8,128)(2,1)} %all_to_all.20.x.surge_ref, bf16[32,128,128]{2,1,0:T(8,128)(2,1)} %get-tuple-element.38.turned_ref, bf16[16,768,256]{2,1,0:T(8,128)(2,1)} %get-tuple-element.34.w0_ref.w1_ref.w2_ref, bf16[16,768,256]{2,1,0:T(8,128)(2,1)} %get-tuple-element.34.w0_ref.w1_ref.w2_ref, ...), custom_call_target="tpu_custom_call" | custom-call | flops 20000000000 | bytes 14680064 | tf_op jit(solution)/shard_map/attention_grads/pallas_call | solution.py:553
  111.8 7.7 %all-to-all-start.2 = ((bf16[32,256,128]{2,1,0:T(8,128)(2,1)}), bf16[32,256,128]{2,1,0:T(8,128)(2,1)S(1)}, u32[]{:S(2)}, u32[]{:S(2)}) async-start(bf16[32,256,128]{2,1,0:T(8,128)(2,1)} %attention_grads.1), calls=%async_computation.2 | async-start | bytes 4194304 | tf_op jit(solution)/shard_map/all_to_all | solution.py:580
  119.5 23.8 %mix_backward.1 = bf16[32,392,128]{2,1,0:T(8,128)(2,1)} custom-call(s32[1]{0:T(128)} %bitcast.8.index_ref, bf16[32,648,128]{2,1,0:T(8,128)(2,1)} %all_to_all.20.x.surge_ref, bf16[32,648,128]{2,1,0:T(8,128)(2,1)} %all_to_all.20.x.surge_ref, bf16[16,768,256]{2,1,0:T(8,128)(2,1)} %get-tuple-element.34.w0_ref.w1_ref.w2_ref, ...), custom_call_target="tpu_custom_call" | custom-call | flops 20000000000 | bytes 12582912 | tf_op jit(solution)/shard_map/mix_backward/pallas_call | solution.py:449
  143.2 0.3 all-to-all-done.2.refs_0_
  143.6 47.5 %all_to_all.21.refs_1_ = bf16[32,392,128]{2,1,0:T(8,128)(2,1)S(1)} all-to-all(bf16[32,392,128]{2,1,0:T(8,128)(2,1)} %mix_backward.1), channel_id=1, replica_groups=mesh['seq'=32,'dp'=4] {'seq'}, dimensions={0} | all-to-all | bytes 6422528 | tf_op jit(solution)/shard_map/all_to_all | solution.py:580
  191.0 0.1 fusion.1
  191.1 3.2 %collective-permute-start = (f32[2,32,128]{2,1,0:T(8,128)S(1)}, f32[2,32,128]{2,1,0:T(8,128)S(1)}, u32[]{:S(2)}, u32[]{:S(2)}) collective-permute-start(f32[2,32,128]{2,1,0:T(8,128)S(1)} %pad_maximum_fusion), channel_id=1, source_target_pairs={{0,1},{1,0},{2,3},{3,2},{4,5},{5,4},{6,7},{7,6},{8,9},{9,8},{10,11... | collective-permute-start | bytes 98312 | tf_op jit(solution)/shard_map/ppermute | solution.py:628
  194.3 0.9 collective-permute-done
  195.2 3.3 %collective-permute-start.1 = (f32[2,32,128]{2,1,0:T(8,128)S(1)}, f32[2,32,128]{2,1,0:T(8,128)S(1)}, u32[]{:S(2)}, u32[]{:S(2)}) collective-permute-start(f32[2,32,128]{2,1,0:T(8,128)S(1)} %fusion), channel_id=1, source_target_pairs={{0,2},{1,3},{2,0},{3,1},{4,6},{5,7},{6,4},{7,5},{8,10},{9,11},{10,... | collective-permute-start | bytes 98312 | tf_op jit(solution)/shard_map/ppermute | solution.py:628
  198.5 3.0 %unpack.1 = (bf16[128,4096]{1,0:T(8,128)(2,1)}, bf16[128,4096]{1,0:T(8,128)(2,1)}, bf16[128,4096]{1,0:T(8,128)(2,1)}, bf16[128,4096]{1,0:T(8,128)(2,1)}, bf16[128,4096]{1,0:T(8,128)(2,1)}) custom-call(bf16[32,256,128]{2,1,0:T(8,128)(2,1)S(1)} %all-to-all-done.2.refs_0_, bf16[32,392,128]{2,1,0:T(8,128)(2,1)S(1)} %all_to_all.21.refs_1_), custom_call_target="tpu_custom_call" | custom-call | bytes 10485760 | tf_op jit(solution)/shard_map/unpack/pallas_call | solution.py:172
  201.5 0.0 collective-permute-done.1
  201.6 0.6 slice_bitcast_fusion
  (5 shorter events, 0.0 us)
Async XLA Ops:
  79.1 22.3 %all-to-all-start.1 = ((bf16[32,128,128]{2,1,0:T(8,128)(2,1)}), bf16[32,128,128]{2,1,0:T(8,128)(2,1)}, u32[]{:S(2)}, u32[]{:S(2)}) async-start(bf16[32,128,128]{2,1,0:T(8,128)(2,1)} %get-tuple-element.35), calls=%async_computation.1 | async-start | bytes 2097152 | tf_op jit(solution)/shard_map/all_to_all | solution.py:580
  111.8 31.8 %all-to-all-start.2 = ((bf16[32,256,128]{2,1,0:T(8,128)(2,1)}), bf16[32,256,128]{2,1,0:T(8,128)(2,1)S(1)}, u32[]{:S(2)}, u32[]{:S(2)}) async-start(bf16[32,256,128]{2,1,0:T(8,128)(2,1)} %attention_grads.1), calls=%async_computation.2 | async-start | bytes 4194304 | tf_op jit(solution)/shard_map/all_to_all | solution.py:580
  191.1 4.1 %collective-permute-start = (f32[2,32,128]{2,1,0:T(8,128)S(1)}, f32[2,32,128]{2,1,0:T(8,128)S(1)}, u32[]{:S(2)}, u32[]{:S(2)}) collective-permute-start(f32[2,32,128]{2,1,0:T(8,128)S(1)} %pad_maximum_fusion), channel_id=1, source_target_pairs={{0,1},{1,0},{2,3},{3,2},{4,5},{5,4},{6,7},{7,6},{8,9},{9,8},{10,11... | collective-permute-start | bytes 98312 | tf_op jit(solution)/shard_map/ppermute | solution.py:628
  195.2 6.3 %collective-permute-start.1 = (f32[2,32,128]{2,1,0:T(8,128)S(1)}, f32[2,32,128]{2,1,0:T(8,128)S(1)}, u32[]{:S(2)}, u32[]{:S(2)}) collective-permute-start(f32[2,32,128]{2,1,0:T(8,128)S(1)} %fusion), channel_id=1, source_target_pairs={{0,2},{1,3},{2,0},{3,1},{4,6},{5,7},{6,4},{7,5},{8,10},{9,11},{10,... | collective-permute-start | bytes 98312 | tf_op jit(solution)/shard_map/ppermute | solution.py:628

commit v4 on v3

--- a/solution.py
+++ b/solution.py
@@ -624,10 +624,12 @@
         [parts[:, 0] + parts[:, 1] + parts[:, 2], parts[:, 3] + parts[:, 4] + parts[:, 5]]
     )
     group = lax.axis_size("dp")
-    for bit in range(group.bit_length() - 1):
-        sums = sums + lax.ppermute(sums, "dp", [(i, i ^ (1 << bit)) for i in range(group)])
+    other = lax.ppermute(sums, "dp", [(i, i ^ 1) for i in range(group)])
+    other, (dq, dk) = lax.optimization_barrier((other, unpack((att_back,), (2,))))
+    sums = sums + other
+    sums = sums + lax.ppermute(sums, "dp", [(i, i ^ 2) for i in range(group)])
     adjoints = sums * positions ** (-0.5)
-    dq, dk, dr, dmk, dmv = unpack((att_back, mix_back), (2, 3))
+    dr, dmk, dmv = unpack((mix_back,), (3,))
     return (dq[None], dk[None], dr[None], dmk[None], dmv[None], adjoints[0], adjoints[1])
 
 

time: 203 us -> 202 us (level)
  transfers between devices with their start and end apart: 4 -> 4, of which waited for: 2 -> 1; matrix products, arithmetic and copies ran while one was open for 0% -> 0% of each run, Pallas kernels for 22% -> 22%
where the time goes in v4:
time: 202 us
  blocking collectives  119 us (59%)
  Pallas kernels  61.9 us (31%)
  starting transfers between devices  18.9 us (9%)
    all_to_all x2, blocking collectives, exchange(): return lax.all_to_all(blocks, 'seq', 0, 0, tiled=True)  119 us
    pallas_call x1, Pallas kernels, mix_backward(): pl.pallas_call(kernel, grid=(steps,), in_specs=[smem(), pl.BlockSpec((per...  23.8 us
    pallas_call x1, Pallas kernels, forward(): pl.pallas_call(kernel, grid=(blocks // per,), in_specs=[smem(), pl.BlockS...  17.6 us
    all_to_all x2, starting transfers between devices, exchange(): return lax.all_to_all(blocks, 'seq', 0, 0, tiled=True)  12.3 us
    pallas_call x1, Pallas kernels, attention_grads(): pl.pallas_call(kernel, grid=(steps,), in_specs=[pl.BlockSpec((group, B, B...  10.4 us
    pallas_call x1, Pallas kernels, pack(): pl.pallas_call(kernel, in_specs=[hbm] * count + [vmem()], out_specs=[hbm,...  6.54 us
  transfers between devices with their start and end apart: 4, of which 1 were waited for; matrix products, arithmetic and copies ran while one was open for 0% of the time, Pallas kernels for 22%

profile of v4, /device:TPU:1, one launch (start us, length us, event | category | flops | bytes accessed | tf_op | source)
XLA Modules:
  0.0 202.0 jit_solution(9545736634574515174)
XLA Ops:
  0.6 6.5 %pack.1 = (bf16[32,648,128]{2,1,0:T(8,128)(2,1)}, bf16[32,128,128]{2,1,0:T(8,128)(2,1)}) custom-call(bf16[128,4096]{1,0:T(8,128)(2,1)} %bitcast.25, bf16[128,4096]{1,0:T(8,128)(2,1)} %bitcast.26, bf16[128,4096]{1,0:T(8,128)(2,1)} %bitcast.27, bf16[128,4096]{1,0:T(8,128)(2,1)} %bitcast.28, bf16[128,4096]{1,0:T(8,128)(2,1)} %bitcast.29, ...), custom_call_target="tpu_custom_call" | custom-call | bytes 12713984 | tf_op jit(solution)/shard_map/pack/pallas_call | solution.py:138
  7.2 71.9 %all_to_all.20.x.surge_ref = bf16[32,648,128]{2,1,0:T(8,128)(2,1)} all-to-all(bf16[32,648,128]{2,1,0:T(8,128)(2,1)} %get-tuple-element.34), channel_id=1, replica_groups=mesh['seq'=32,'dp'=4] {'seq'}, dimensions={0} | all-to-all | bytes 10616832 | tf_op jit(solution)/shard_map/all_to_all | solution.py:580
  79.1 4.7 %all-to-all-start.1 = ((bf16[32,128,128]{2,1,0:T(8,128)(2,1)}), bf16[32,128,128]{2,1,0:T(8,128)(2,1)}, u32[]{:S(2)}, u32[]{:S(2)}) async-start(bf16[32,128,128]{2,1,0:T(8,128)(2,1)} %get-tuple-element.38), calls=%async_computation.1 | async-start | bytes 2097152 | tf_op jit(solution)/shard_map/all_to_all | solution.py:580
  83.8 17.6 %forward.1 = (bf16[32,128,128]{2,1,0:T(8,128)(2,1)}, f32[32,128,128]{2,1,0:T(8,128)}, f32[32,128,128]{2,1,0:T(8,128)}, bf16[16,768,256]{2,1,0:T(8,128)(2,1)}, bf16[32,128,128]{2,1,0:T(8,128)(2,1)}) custom-call(s32[1]{0:T(128)} %bitcast.8.index_ref, bf16[32,648,128]{2,1,0:T(8,128)(2,1)} %all_to_all.20.x.surge_ref, f32[32,128]{1,0:T(8,128)} %fading_ref.3, ...), custom_call_target="tpu_custom_call" | custom-call | flops 20000000000 | bytes 18874368 | tf_op jit(solution)/shard_map/forward/pallas_call | solution.py:314
  101.3 0.0 all-to-all-done.1.cot_ref
  101.3 10.4 %attention_grads.1 = bf16[32,256,128]{2,1,0:T(8,128)(2,1)} custom-call(bf16[32,648,128]{2,1,0:T(8,128)(2,1)} %all_to_all.20.x.surge_ref, bf16[32,128,128]{2,1,0:T(8,128)(2,1)} %get-tuple-element.41.turned_ref, bf16[16,768,256]{2,1,0:T(8,128)(2,1)} %get-tuple-element.37.w0_ref.w1_ref.w2_ref, bf16[16,768,256]{2,1,0:T(8,128)(2,1)} %get-tuple-element.37.w0_ref.w1_ref.w2_ref, ...), custom_call_target="tpu_custom_call" | custom-call | flops 20000000000 | bytes 14680064 | tf_op jit(solution)/shard_map/attention_grads/pallas_call | solution.py:553
  111.8 7.7 %all-to-all-start.2 = ((bf16[32,256,128]{2,1,0:T(8,128)(2,1)}), bf16[32,256,128]{2,1,0:T(8,128)(2,1)S(1)}, u32[]{:S(2)}, u32[]{:S(2)}) async-start(bf16[32,256,128]{2,1,0:T(8,128)(2,1)} %attention_grads.1), calls=%async_computation.2 | async-start | bytes 4194304 | tf_op jit(solution)/shard_map/all_to_all | solution.py:580
  119.4 23.8 %mix_backward.1 = bf16[32,392,128]{2,1,0:T(8,128)(2,1)} custom-call(s32[1]{0:T(128)} %bitcast.8.index_ref, bf16[32,648,128]{2,1,0:T(8,128)(2,1)} %all_to_all.20.x.surge_ref, bf16[32,648,128]{2,1,0:T(8,128)(2,1)} %all_to_all.20.x.surge_ref, bf16[16,768,256]{2,1,0:T(8,128)(2,1)} %get-tuple-element.37.w0_ref.w1_ref.w2_ref, ...), custom_call_target="tpu_custom_call" | custom-call | flops 20000000000 | bytes 12582912 | tf_op jit(solution)/shard_map/mix_backward/pallas_call | solution.py:449
  143.2 0.3 all-to-all-done.2.refs_0_
  143.5 47.5 %all_to_all.21.refs_0_ = bf16[32,392,128]{2,1,0:T(8,128)(2,1)S(1)} all-to-all(bf16[32,392,128]{2,1,0:T(8,128)(2,1)} %mix_backward.1), channel_id=1, replica_groups=mesh['seq'=32,'dp'=4] {'seq'}, dimensions={0} | all-to-all | bytes 6422528 | tf_op jit(solution)/shard_map/all_to_all | solution.py:580
  191.0 0.1 fusion.1
  191.1 3.2 %collective-permute-start = (f32[2,32,128]{2,1,0:T(8,128)S(1)}, f32[2,32,128]{2,1,0:T(8,128)S(1)}, u32[]{:S(2)}, u32[]{:S(2)}) collective-permute-start(f32[2,32,128]{2,1,0:T(8,128)S(1)} %pad_maximum_fusion), channel_id=1, source_target_pairs={{0,1},{1,0},{2,3},{3,2},{4,5},{5,4},{6,7},{7,6},{8,9},{9,8},{10,11... | collective-permute-start | bytes 98312 | tf_op jit(solution)/shard_map/ppermute | solution.py:627
  194.3 1.6 unpack.2
  195.9 0.0 collective-permute-done
  195.9 3.4 %collective-permute-start.1 = (f32[2,32,128]{2,1,0:T(8,128)S(1)}, f32[2,32,128]{2,1,0:T(8,128)S(1)}, u32[]{:S(2)}, u32[]{:S(2)}) collective-permute-start(f32[2,32,128]{2,1,0:T(8,128)S(1)} %fusion), channel_id=1, source_target_pairs={{0,2},{1,3},{2,0},{3,1},{4,6},{5,7},{6,4},{7,5},{8,10},{9,11},{10,... | collective-permute-start | bytes 98312 | tf_op jit(solution)/shard_map/ppermute | solution.py:630
  199.3 2.1 %unpack.3 = (bf16[128,4096]{1,0:T(8,128)(2,1)}, bf16[128,4096]{1,0:T(8,128)(2,1)}, bf16[128,4096]{1,0:T(8,128)(2,1)}) custom-call(bf16[32,392,128]{2,1,0:T(8,128)(2,1)S(1)} %all_to_all.21.refs_0_), custom_call_target="tpu_custom_call" | custom-call | bytes 6291456 | tf_op jit(solution)/shard_map/unpack/pallas_call | solution.py:172
  201.4 0.0 collective-permute-done.1
  201.4 0.6 slice_bitcast_fusion
  (5 shorter events, 0.0 us)
Async XLA Ops:
  79.1 22.2 %all-to-all-start.1 = ((bf16[32,128,128]{2,1,0:T(8,128)(2,1)}), bf16[32,128,128]{2,1,0:T(8,128)(2,1)}, u32[]{:S(2)}, u32[]{:S(2)}) async-start(bf16[32,128,128]{2,1,0:T(8,128)(2,1)} %get-tuple-element.38), calls=%async_computation.1 | async-start | bytes 2097152 | tf_op jit(solution)/shard_map/all_to_all | solution.py:580
  111.8 31.8 %all-to-all-start.2 = ((bf16[32,256,128]{2,1,0:T(8,128)(2,1)}), bf16[32,256,128]{2,1,0:T(8,128)(2,1)S(1)}, u32[]{:S(2)}, u32[]{:S(2)}) async-start(bf16[32,256,128]{2,1,0:T(8,128)(2,1)} %attention_grads.1), calls=%async_computation.2 | async-start | bytes 4194304 | tf_op jit(solution)/shard_map/all_to_all | solution.py:580
  191.1 4.8 %collective-permute-start = (f32[2,32,128]{2,1,0:T(8,128)S(1)}, f32[2,32,128]{2,1,0:T(8,128)S(1)}, u32[]{:S(2)}, u32[]{:S(2)}) collective-permute-start(f32[2,32,128]{2,1,0:T(8,128)S(1)} %pad_maximum_fusion), channel_id=1, source_target_pairs={{0,1},{1,0},{2,3},{3,2},{4,5},{5,4},{6,7},{7,6},{8,9},{9,8},{10,11... | collective-permute-start | bytes 98312 | tf_op jit(solution)/shard_map/ppermute | solution.py:627
  195.9 5.4 %collective-permute-start.1 = (f32[2,32,128]{2,1,0:T(8,128)S(1)}, f32[2,32,128]{2,1,0:T(8,128)S(1)}, u32[]{:S(2)}, u32[]{:S(2)}) collective-permute-start(f32[2,32,128]{2,1,0:T(8,128)S(1)} %fusion), channel_id=1, source_target_pairs={{0,2},{1,3},{2,0},{3,1},{4,6},{5,7},{6,4},{7,5},{8,10},{9,11},{10,... | collective-permute-start | bytes 98312 | tf_op jit(solution)/shard_map/ppermute | solution.py:630
